TPU v7x, 32 devices: a whole 2x2x4 slice. The times are simulated.
32 devices in a mesh: groups: 2 (over y), row: 8 (over z, x), col: 2 (over core).
Axes of the slice: x: 2, y: 2, z: 4, core: 2. Of those that a mesh axis runs over, the one named last changes fastest.
Arguments:
- slab: float32 [24576, 512], P(('groups', 'row', 'col')), parts along dimension 0, may hold values from -6 to 6
- predictors: float32 [1024, 256], P(('groups', 'row', 'col')), parts along dimension 0, may hold values from -6 to 6
Outputs:
- covariance: float32 [24576, 12288], P(('groups', 'row'), 'col'), parts along dimension 0
There are 2 independent parts, one for each index of `groups`. A program takes and returns all parts, laid end to end along the dimension named above; each array names one. Nothing has to cross between parts.
All inputs are finite; a program needn't handle non-finite values.
Results may differ from a plain program's by a relative error of at most 0.000078.
Values sent between devices are 32-bit elements; how exact they have to be, the bound alone decides.
No kernel may reach another device: no remote copies, remote signals or barrier semaphores. Data moves between devices by JAX's collectives and lax.ppermute only.
A program may use at most 192 MiB of HBM per device.

v0:
```python
import functools

import jax
import jax.numpy as jnp
import numpy as np
from jax import lax
from jax.experimental import pallas as pl
from jax.experimental.pallas import tpu as pltpu
from jax.sharding import PartitionSpec as P


f32, bf16 = jnp.float32, jnp.bfloat16
AXES = ("row", "col")
NN = (((1,), (0,)), ((), ()))
TN = (((0,), (0,)), ((), ()))
NT = (((1,), (1,)), ((), ()))
TT = (((0,), (1,)), ((), ()))


def low(a, b, dims=NN):
    return lax.dot_general(a.astype(bf16), b.astype(bf16), dims, preferred_element_type=f32)


def halves(a):
    h = a.astype(bf16)
    return h, (a - h.astype(f32)).astype(bf16)


def mid(a, b, dims=NN):
    ah, al = halves(a)
    bh, bl = halves(b)
    dot = functools.partial(lax.dot_general, dimension_numbers=dims, preferred_element_type=f32)
    return dot(ah, bh) + (dot(ah, bl) + dot(al, bh))


def high(a, b, dims=NN):
    return lax.dot_general(a, b, dims, precision=lax.Precision.HIGHEST, preferred_element_type=f32)


def eye(n):
    r = lax.broadcasted_iota(jnp.int32, (n, n), 0)
    c = lax.broadcasted_iota(jnp.int32, (n, n), 1)
    return jnp.where(r == c, 1.0, 0.0).astype(f32)


def basis_kernel(count, spots, *refs):
    parts, (c_ref, x_ref, g_ref, v_ref, b_ref, z_ref, s_ref, e_ref) = refs[:count], refs[count:]
    m, n = x_ref.shape
    blocks, size = parts[0].shape[:2]
    for i, part in enumerate(parts):
        for j in range(blocks):
            if count * blocks == 1:
                x_ref[...] = part[j]
            else:
                at = pick(spots[:, i * blocks + j])
                x_ref[pl.ds(pl.multiple_of(at * size, size), size), :] = part[j]
    x = x_ref[...]
    ident = eye(n)
    gram = high(x, x, TN)
    bound = jnp.max(jnp.sum(jnp.abs(gram), axis=0, keepdims=True))
    g = gram / bound
    g_ref[...] = g
    v = 3.4445 * ident - 4.7750 * g + 2.0315 * low(g, g)
    k = low(v, low(g, v))
    v = 3.4445 * v - low(v, 4.7750 * k - 2.0315 * low(k, k))
    for _ in range(2):
        k = ident - low(v, low(g, v))
        v = v + low(v, 0.5 * k + 0.375 * low(k, k))
    v_ref[...] = v

    def polish(dot=high):
        v = v_ref[...]
        k = ident - dot(v, dot(g_ref[...], v), TN)
        k2 = low(k, k)
        v_ref[...] = v + mid(v, 0.5 * k + 0.375 * k2 + 0.3125 * low(k, k2))
        return jnp.max(jnp.abs(k))

    polish(mid)
    lax.while_loop(
        lambda at: jnp.logical_and(at[0] < 60, jnp.logical_not(at[1] < 1e-4)),
        lambda at: (at[0] + 1, polish()),
        (jnp.int32(0), polish()),
    )
    v = v_ref[...] * lax.rsqrt(bound)
    v_ref[...] = v
    q1 = high(x, v)
    a = q1[:n]
    s = jnp.where(jnp.sum(a * ident, axis=0, keepdims=True) < 0, 1.0, -1.0).astype(f32)
    s_ref[...] = s
    p = low(v, x[:n], TT) * s
    b_ref[...] = ident - high(v, x[:n], TT) * s
    z = ident + p
    for _ in range(4):
        p = low(p, p)
        z = z + low(z, p)
    z_ref[...] = z

    def refine(dot=high):
        z = z_ref[...]
        k = ident - dot(b_ref[...], z)
        z_ref[...] = z + mid(z, k + low(k, k))
        return jnp.max(jnp.abs(k))

    refine(mid)
    error = refine()

    @pl.when(jnp.logical_not(error < 3e-5))
    def _():
        e_ref[...] = high(x_ref[:n], v_ref[...])
        rows = lax.broadcasted_iota(jnp.int32, (n, n), 0)
        cols = lax.broadcasted_iota(jnp.int32, (n, n), 1)
        lane = lax.broadcasted_iota(jnp.int32, (1, n), 1)

        def step(j, s):
            e = e_ref[...]
            row = jnp.sum(jnp.where(rows == j, e, 0.0), axis=0, keepdims=True)
            col = jnp.sum(jnp.where(cols == j, e, 0.0), axis=1, keepdims=True)
            head = jnp.sum(jnp.where(lane == j, row, 0.0), axis=1, keepdims=True)
            sign = jnp.where(head < 0, 1.0, -1.0)
            col = jnp.where(rows[:, :1] > j, col / (head - sign), 0.0)
            e_ref[...] = e - col * jnp.where(lane == j, row - sign, row)
            return jnp.where(lane == j, sign, s)

        s = lax.fori_loop(0, n, step, jnp.zeros((1, n), f32))
        s_ref[...] = s
        b = eye(n) - high(v_ref[...], x_ref[:n], TT) * s
        b_ref[...] = b
        z_ref[...] = 0.49 * b.T
        lax.while_loop(
            lambda at: jnp.logical_and(at[0] < 60, jnp.logical_not(at[1] < 3e-5)),
            lambda at: (at[0] + 1, refine()),
            (jnp.int32(0), refine()),
        )
        refine()

    q2 = q1[n:]
    nt = -high(q2, z_ref[...], NT)
    c_ref[:, :n] = high(nt, a - ident * s_ref[...], NT)
    c_ref[:, n:] = eye(m - n) + high(nt, q2, NT)


def basis(parts, spots):
    blocks, size, n = parts[0].shape
    m = len(parts) * blocks * size
    return pl.pallas_call(
        functools.partial(basis_kernel, len(parts), spots),
        out_shape=jax.ShapeDtypeStruct((m - n, m), f32),
        in_specs=[pl.BlockSpec(memory_space=pltpu.VMEM)] * len(parts),
        out_specs=pl.BlockSpec(memory_space=pltpu.VMEM),
        scratch_shapes=[pltpu.VMEM((m, n), f32)]
        + [pltpu.VMEM((n, n), f32)] * 4
        + [pltpu.VMEM((1, n), f32), pltpu.VMEM((n, n), f32)],
        compiler_params=pltpu.CompilerParams(vmem_limit_bytes=24 << 20),
        cost_estimate=pl.CostEstimate(flops=8_000_000_000, bytes_accessed=1 << 20, transcendentals=0),
        name="basis",
    )(*parts)


def pick(column):
    device = lax.axis_index("row") * lax.axis_size("col") + lax.axis_index("col")
    value = jnp.int32(int(column[0]))
    for d in range(1, len(column)):
        if column[d] != column[0]:
            value = jnp.where(device == d, jnp.int32(int(column[d])), value)
    return value


def beside(*parts):
    return jnp.concatenate(parts, axis=1)


def project_kernel(count, c_ref, *refs):
    pieces, outs, (held, sem) = refs[:count], refs[count:2 * count], refs[2 * count:]
    for i in range(count):
        pltpu.make_async_copy(pieces[i], held.at[i], sem.at[i]).start()
    ch, cl = halves(c_ref[...])
    cat = beside(ch, cl, ch)
    for i in range(count):
        pltpu.make_async_copy(pieces[i], held.at[i], sem.at[i]).wait()
        h, l = halves(held[i])
        outs[i][...] = lax.dot_general(cat, beside(h, h, l), NT, preferred_element_type=f32)


def project(comp, pieces):
    count = len(pieces)
    shard, samples = pieces[0].shape
    k = comp.shape[0]
    return pl.pallas_call(
        functools.partial(project_kernel, count),
        out_shape=[jax.ShapeDtypeStruct((k, shard), f32)] * count,
        in_specs=[pl.BlockSpec(memory_space=pltpu.VMEM)] + [pl.BlockSpec(memory_space=pltpu.HBM)] * count,
        out_specs=[pl.BlockSpec(memory_space=pltpu.VMEM)] * count,
        scratch_shapes=[pltpu.VMEM((count, shard, samples), f32), pltpu.SemaphoreType.DMA((count,))],
        compiler_params=pltpu.CompilerParams(vmem_limit_bytes=24 << 20),
        cost_estimate=pl.CostEstimate(
            flops=6 * count * shard * samples * k, bytes_accessed=4 * count * shard * (samples + k), transcendentals=0
        ),
        name="project",
    )(comp, *pieces)


def own_kernel(c_ref, mine_ref, theirs_ref, rows_ref, b_ref, held, sem):
    core = lax.axis_index("col")
    shard, samples = held.shape[1:]
    for i, ref in enumerate((mine_ref, theirs_ref)):
        pltpu.make_async_copy(ref, held.at[i], sem.at[i]).start()
    ch, cl = halves(c_ref[...])
    left, right = beside(ch, cl, ch), beside(ch, ch, cl)
    for i, ref in enumerate((mine_ref, theirs_ref)):
        pltpu.make_async_copy(ref, held.at[i], sem.at[i]).wait()
        h, l = halves(held[i])
        if i == 1:
            b_ref[...] = lax.dot_general(left, beside(h, h, l), NT, preferred_element_type=f32)
        w = lax.dot_general(beside(h, l, h), right, NT, preferred_element_type=f32) * (1.0 / samples)
        h, l = halves(w)
        at = pl.ds(pl.multiple_of((core if i == 0 else 1 - core) * shard, shard), shard)
        rows_ref[at, :] = beside(h, l, h)


def own_parts(comp, mine, theirs):
    shard, samples = mine.shape
    k = comp.shape[0]
    return pl.pallas_call(
        own_kernel,
        out_shape=[jax.ShapeDtypeStruct((2 * shard, 3 * k), bf16), jax.ShapeDtypeStruct((k, shard), f32)],
        in_specs=[pl.BlockSpec(memory_space=pltpu.VMEM)] + [pl.BlockSpec(memory_space=pltpu.HBM)] * 2,
        out_specs=[pl.BlockSpec(memory_space=pltpu.VMEM)] * 2,
        scratch_shapes=[pltpu.VMEM((2, shard, samples), f32), pltpu.SemaphoreType.DMA((2,))],
        compiler_params=pltpu.CompilerParams(vmem_limit_bytes=24 << 20),
        cost_estimate=pl.CostEstimate(
            flops=18 * shard * samples * k, bytes_accessed=8 * shard * (samples + 2 * k), transcendentals=0
        ),
        name="own",
    )(comp, mine, theirs)


def tiles_kernel(parts, plan, given, rows_ref, *refs):
    count, turns = sum(parts), plan.shape[1] // 2
    pieces, refs = refs[:count], refs[count + (1 if given else 0):]
    out_ref, held, cat, tile, in_sem, out_sem = refs
    k, shard = held.shape[1:]
    height = tile.shape[2]
    steps = rows_ref.shape[0] // height
    which = [pick(plan[:, 2 * t]) for t in range(turns)]
    slots = [pick(plan[:, 2 * t + 1]) for t in range(turns)]

    def store(turn, t):
        cols = pl.ds(pl.multiple_of(slots[turn] * shard, shard), shard)
        return pltpu.make_async_copy(
            tile.at[turn, t], out_ref.at[pl.ds(t * height, height), cols], out_sem.at[turn, t]
        )

    for turn in range(turns):
        at = 0
        for i, n in enumerate(parts):
            if (plan[:, 2 * turn] == i).any():
                @pl.when(which[turn] == i)
                def _():
                    for j in range(n):
                        into = held.at[turn, pl.ds(j * (k // n), k // n)]
                        pltpu.make_async_copy(pieces[at + j], into, in_sem.at[turn]).start()
            at += n

    for turn in range(turns):
        @pl.when(which[turn] >= 0)
        def _():
            pltpu.make_async_copy(held.at[turn], held.at[turn], in_sem.at[turn]).wait()
            h, l = halves(held[turn])
            cat[:k] = h
            cat[k:2 * k] = h
            cat[2 * k:] = l
            for t in range(steps):
                lhs = rows_ref[t * height:(t + 1) * height, :]
                tile[turn, t] = lax.dot_general(lhs, cat[...], NN, preferred_element_type=f32)
                store(turn, t).start()

    for turn in range(turns):
        @pl.when(which[turn] >= 0)
        def _():
            for t in range(steps):
                store(turn, t).wait()


def tiles(plan, rows, pieces, out, width):
    turns = plan.shape[1] // 2
    k, shard = rows.shape[1] // 3, pieces[0][0].shape[1]
    arrays = [w for piece in pieces for w in piece]
    steps = 3 if rows.shape[0] % 48 == 0 else 2
    height = rows.shape[0] // steps
    given = [] if out is None else [out]
    return pl.pallas_call(
        functools.partial(tiles_kernel, [len(piece) for piece in pieces], plan, out is not None),
        out_shape=jax.ShapeDtypeStruct((rows.shape[0], width), f32),
        in_specs=[pl.BlockSpec(memory_space=pltpu.VMEM)] + [pl.BlockSpec(memory_space=pl.ANY)] * (len(arrays) + len(given)),
        out_specs=pl.BlockSpec(memory_space=pl.ANY),
        scratch_shapes=[
            pltpu.VMEM((turns, k, shard), f32),
            pltpu.VMEM((3 * k, shard), bf16),
            pltpu.VMEM((turns, steps, height, shard), f32),
            pltpu.SemaphoreType.DMA((turns,)),
            pltpu.SemaphoreType.DMA((turns, steps)),
        ],
        input_output_aliases={1 + len(arrays): 0} if given else {},
        compiler_params=pltpu.CompilerParams(vmem_limit_bytes=28 << 20),
        cost_estimate=pl.CostEstimate(
            flops=turns * rows.shape[0] * shard * k * 6, bytes_accessed=turns * rows.shape[0] * shard * 4, transcendentals=0
        ),
        name="tiles",
    )(rows, *arrays, *given)


def gather_all(x, n_row, n_col):
    n = n_row * n_col
    if n & (n - 1) or n_col != 2 or n < 8 or x.shape[0] % 8:
        return [lax.all_gather(x, AXES, axis=0, tiled=True)[None]], np.zeros((n, 1), np.int32)
    y, held = x[None], [0]
    bit = n_col
    while 2 * bit < n:
        other = lax.ppermute(y, AXES, [(i, i ^ bit) for i in range(n)])
        y, held = jnp.concatenate([y, other]), held + [h ^ bit for h in held]
        bit *= 2
    parts, spots = [y], list(held)
    for flip in (bit, 1, bit + 1):
        source = parts[1] if flip == bit + 1 else y
        parts.append(lax.ppermute(source, AXES, [(i, i ^ (1 if flip & 1 else flip)) for i in range(n)]))
        spots += [h ^ flip for h in held]
    return parts, np.array([[i ^ h for h in spots] for i in range(n)], np.int32)


def ring_of(mesh):
    n = mesh.shape["row"]
    at = [getattr(d, "coords", None) for d in mesh.devices[0, :, 0]]
    if any(c is None for c in at):
        return list(range(n))
    axes = [sorted({c[i] for c in at}) for i in range(3)]
    wide = [i for i in range(3) if len(axes[i]) > 1]
    index = {tuple(c): r for r, c in enumerate(at)}
    if len(wide) != 2 or len(index) != n or n != len(axes[wide[0]]) * len(axes[wide[1]]):
        return list(range(n))
    if len(axes[wide[0]]) % 2:
        wide.reverse()
    lines, places = axes[wide[0]], axes[wide[1]]

    def row(line, place):
        c = list(at[0])
        c[wide[0]], c[wide[1]] = line, place
        return index[tuple(c)]

    order = [row(lines[0], places[0])]
    for i, line in enumerate(lines):
        order += [row(line, p) for p in (places[1:] if i % 2 == 0 else places[:0:-1])]
    return order + [row(line, places[0]) for line in lines[:0:-1]]


def shards(ring, slab, predictors):
    return covariance(ring, slab, predictors)


def covariance(ring, slab, predictors):
    n_row, n_col = lax.axis_size("row"), lax.axis_size("col")
    shard, samples = slab.shape
    width = n_row * shard

    if n_col != 2 or n_row % 2 or shard % 128:
        comp = basis(*gather_all(predictors, n_row, n_col))
        w = lax.dot_general(slab, comp, NT, precision=lax.Precision.HIGHEST)
        every = lax.all_gather(w, AXES, axis=0, tiled=True)
        cols = lax.dynamic_slice_in_dim(every, lax.axis_index("col") * width, width)
        rows = lax.dynamic_slice_in_dim(every, lax.axis_index("row") * n_col * shard, n_col * shard)
        return jnp.dot(rows * (1.0 / samples), cols.T, precision=lax.Precision.HIGHEST)

    home = [i * n_col // n_row for i in range(n_row)]
    place = {i: p for p, i in enumerate(ring)}

    def hop(x, way, steps, source=None):
        pairs = []
        for q in range(n_row):
            a, b = ring[(q + way * (steps - 1)) % n_row], ring[(q + way * steps) % n_row]
            h = home[ring[q]]
            pairs.append((a * n_col + (h if source is None else source), b * n_col + h))
        return lax.ppermute(x, AXES, pairs)

    todo = [[[] for _ in range(n_row * n_col)], {}]

    def arrive(offset, core, w):
        key = (offset, core)
        todo[1][key] = w
        for r in range(n_row):
            for c in range(n_col):
                q = ring[(place[r] + offset) % n_row]
                if home[q] == c:
                    e = {"mine": c, "theirs": 1 - c}.get(core, core)
                    todo[0][r * n_col + c].append((key, (q - c * (n_row // n_col)) * n_col + e))

    def work(rows, out, turns=2):
        turns = min(turns, max(len(t) for t in todo[0]))
        if turns == 0:
            return out
        table, names = np.full((n_row * n_col, 2 * turns), -1, np.int32), []
        for d, waiting in enumerate(todo[0]):
            for i in range(min(turns, len(waiting))):
                key, slot = waiting.pop(0)
                if key not in names:
                    names.append(key)
                table[d, 2 * i:2 * i + 2] = names.index(key), slot
        return tiles(table, rows, [todo[1][key] for key in names], out, width)

    half = n_row // 2
    near = {way: hop(slab, way, 1, 0) for way in (1, -1)}
    other = lax.ppermute(slab, "col", [(0, 1), (1, 0)])
    comp = basis(*gather_all(predictors, n_row, n_col))
    (mine,) = project(comp, [slab])
    flights = [(1, 1, {way: hop(mine, way, 1, 1) for way in (1, -1)})]
    first = dict(zip((1, -1), project(comp, [near[1], near[-1]])))

    def onward(core, steps, sent):
        if steps + 1 < half:
            flights.append((core, steps + 1, {way: hop(sent[way], way, steps + 1) for way in sent}))
        elif steps + 1 == half:
            k = sent[1].shape[0] // 2
            flights.append((core, half, {1: hop(sent[1][:k], 1, half), -1: hop(sent[-1][k:], -1, half)}))

    onward(0, 1, first)
    rows, theirs = own_parts(comp, slab, other)
    arrive(0, "mine", [mine])
    arrive(0, "theirs", [theirs])
    for way in (1, -1):
        arrive(-way, 0, [first[way]])
    out = work(rows, None, 1)
    while flights:
        core, steps, sent = flights.pop(0)
        got = lax.optimization_barrier(tuple(sent.values()) + (out,))
        out = got[-1]
        sent = dict(zip(sent, got))
        onward(core, steps, sent)
        if steps < half:
            for way, w in sent.items():
                arrive(-way * steps, core, [w])
        else:
            arrive(half, core, list(sent.values()))
        out = work(rows, out, (1 if steps + 1 < half else 2) if flights else 8)
    return out


def solution(mesh):
    return jax.shard_map(
        functools.partial(shards, ring_of(mesh)),
        mesh=mesh,
        in_specs=(P(("groups", "row", "col"), None), P(("groups", "row", "col"), None)),
        out_specs=P(("groups", "row"), "col"),
        check_vma=False,
    )
```

profile of v0, /device:TPU:28, one launch (start us, length us, event | category | flops | bytes accessed | tf_op | source)
XLA Modules:
  0.0 129.0 jit_solution(5219746103286682449)
XLA Ops:
  0.0 1.5 %collective-permute-start = (f32[1,32,256]{2,1,0:T(8,128)}, f32[1,32,256]{2,1,0:T(8,128)S(1)}, u32[]{:S(2)}, u32[]{:S(2)}) collective-permute-start(f32[1,32,256]{2,1,0:T(8,128)} %bitcast.1), channel_id=1, source_target_pairs={{0,2},{1,3},{2,0},{3,1},{4,6},{5,7},{6,4},{7,5},{8,10},{9,11},{10,... | collective-permute-start | bytes 98312 | tf_op jit(solution)/shard_map/ppermute | solution.py:319
  1.5 2.6 %collective-permute-done = f32[1,32,256]{2,1,0:T(8,128)S(1)} collective-permute-done((f32[1,32,256]{2,1,0:T(8,128)}, f32[1,32,256]{2,1,0:T(8,128)S(1)}, u32[]{:S(2)}, u32[]{:S(2)}) %collective-permute-start) | collective-permute-done | bytes 32800 | tf_op jit(solution)/shard_map/ppermute | solution.py:319
  5.3 1.5 %collective-permute-start.8 = (f32[768,512]{1,0:T(8,128)}, f32[768,512]{1,0:T(8,128)S(1)}, u32[]{:S(2)}, u32[]{:S(2)}) collective-permute-start(f32[768,512]{1,0:T(8,128)} %refs_0_.1), channel_id=1, source_target_pairs={{0,4},{4,8},{8,13},{12,15},{14,11},{10,7},{6,2},{2,0},{16,20},{20,... | collective-permute-start | bytes 4718600 | tf_op jit(solution)/shard_map/ppermute | solution.py:381
  6.8 1.4 %collective-permute-start.9 = (f32[768,512]{1,0:T(8,128)}, f32[768,512]{1,0:T(8,128)S(1)}, u32[]{:S(2)}, u32[]{:S(2)}) collective-permute-start(f32[768,512]{1,0:T(8,128)} %refs_0_.1), channel_id=1, source_target_pairs={{0,2},{4,0},{8,5},{12,9},{14,13},{10,15},{6,10},{2,6},{16,18},{20,... | collective-permute-start | bytes 4718600 | tf_op jit(solution)/shard_map/ppermute | solution.py:381
  8.3 0.8 collective-permute-done.1
  9.9 2.7 %collective-permute-start.2 = (f32[4,32,256]{2,1,0:T(8,128)S(1)}, f32[4,32,256]{2,1,0:T(8,128)S(1)}, u32[]{:S(2)}, u32[]{:S(2)}) collective-permute-start(f32[4,32,256]{2,1,0:T(8,128)S(1)} %pad_maximum_fusion.refs_0_), channel_id=1, source_target_pairs={{0,8},{1,9},{2,10},{3,11},{4,12},{5,13},{6,14},{7,15},{8,0},{9,1},... | collective-permute-start | bytes 393224 | tf_op jit(solution)/shard_map/ppermute | solution.py:325
  12.8 21.7 %collective-permute-done.2.refs_1_ = f32[4,32,256]{2,1,0:T(8,128)S(1)} collective-permute-done((f32[4,32,256]{2,1,0:T(8,128)S(1)}, f32[4,32,256]{2,1,0:T(8,128)S(1)}, u32[]{:S(2)}, u32[]{:S(2)}) %collective-permute-start.2) | collective-permute-done | bytes 131104 | tf_op jit(solution)/shard_map/ppermute | solution.py:325
  34.5 1.3 %collective-permute-done.4.refs_3_ = f32[4,32,256]{2,1,0:T(8,128)S(1)} collective-permute-done((f32[4,32,256]{2,1,0:T(8,128)S(1)}, f32[4,32,256]{2,1,0:T(8,128)S(1)}, u32[]{:S(2)}, u32[]{:S(2)}) %collective-permute-start.4) | collective-permute-done | bytes 131104 | tf_op jit(solution)/shard_map/ppermute | solution.py:325
  35.8 13.4 %basis.1.c_ref = f32[256,512]{1,0:T(8,128)S(1)} custom-call(f32[4,32,256]{2,1,0:T(8,128)S(1)} %pad_maximum_fusion.refs_0_, f32[4,32,256]{2,1,0:T(8,128)S(1)} %collective-permute-done.2.refs_1_, f32[4,32,256]{2,1,0:T(8,128)S(1)} %collective-permute-done.3.refs_2_, f32[4,32,256]{2,1,0:T(8,128)S(1)} %collective-permute-done.4.refs_3_), custom_call_target="tpu_custom_call" | custom-call | flops 8000000000 | bytes 1048576 | tf_op jit(solution)/shard_map/basis/pallas_call | solution.py:145
  49.3 1.4 %copy-done = f32[768,512]{1,0:T(8,128)S(1)} copy-done((f32[768,512]{1,0:T(8,128)S(1)}, f32[768,512]{1,0:T(8,128)}, u32[]{:S(2)}) %copy-start) | copy-done | bytes 1572888
  50.7 1.0 project.2.refs_0_
  53.2 2.4 %project.3 = (f32[256,768]{1,0:T(8,128)S(1)}, f32[256,768]{1,0:T(8,128)S(1)}) custom-call(f32[256,512]{1,0:T(8,128)S(1)} %basis.1.c_ref, f32[768,512]{1,0:T(8,128)S(1)} %collective-permute-done.8.refs_0_, f32[768,512]{1,0:T(8,128)S(1)} %collective-permute-done.9.refs_1_), custom_call_target="tpu_custom_call" | custom-call | flops 1207959552 | bytes 4718592 | tf_op jit(solution)/shard_map/project/pallas_call | solution.py:188
  56.3 1.3 %collective-permute-start.12 = (f32[256,768]{1,0:T(8,128)S(1)}, f32[256,768]{1,0:T(8,128)S(1)}, u32[]{:S(2)}, u32[]{:S(2)}) collective-permute-start(f32[256,768]{1,0:T(8,128)S(1)} %get-tuple-element.32.refs_2_.refs_0_), channel_id=1, source_target_pairs={{4,8},{8,12},{13,15},{15,11},{11,7},{7,3},{2,0},{0,4},{20,24},{24,... | collective-permute-start | bytes 2359304 | tf_op jit(solution)/shard_map/ppermute | solution.py:381
  57.6 1.4 %copy-done.1 = f32[768,512]{1,0:T(8,128)S(1)} copy-done((f32[768,512]{1,0:T(8,128)S(1)}, f32[768,512]{1,0:T(8,128)}, u32[]{:S(2)}) %copy-start.1) | copy-done | bytes 1572888
  59.0 2.6 %own.1 = (bf16[1536,768]{1,0:T(8,128)(2,1)S(1)}, f32[256,768]{1,0:T(8,128)S(1)}) custom-call(f32[256,512]{1,0:T(8,128)S(1)} %basis.1.c_ref, f32[768,512]{1,0:T(8,128)S(1)} %copy-done.1, f32[768,512]{1,0:T(8,128)S(1)} %collective-permute-done.5.theirs_ref), custom_call_target="tpu_custom_call" | custom-call | flops 1811939328 | bytes 6291456 | tf_op jit(solution)/shard_map/own/pallas_call | solution.py:223
  61.7 1.3 %collective-permute-start.10 = (f32[256,768]{1,0:T(8,128)S(1)}, f32[256,768]{1,0:T(8,128)S(1)}, u32[]{:S(2)}, u32[]{:S(2)}) collective-permute-start(f32[256,768]{1,0:T(8,128)S(1)} %collective-permute-done.6.refs_2_.refs_3_.refs_0_), channel_id=1, source_target_pairs={{4,8},{8,12},{13,15},{15,11},{11,7},{7,3},{2,0},{0,4},{20,24},{24,... | collective-permute-start | bytes 2359304 | tf_op jit(solution)/shard_map/ppermute | solution.py:381
  63.8 9.4 %collective-permute-done.12.refs_2_.refs_4_.refs_0_ = f32[256,768]{1,0:T(8,128)S(1)} collective-permute-done((f32[256,768]{1,0:T(8,128)S(1)}, f32[256,768]{1,0:T(8,128)S(1)}, u32[]{:S(2)}, u32[]{:S(2)}) %collective-permute-start.12) | collective-permute-done | bytes 786464 | tf_op jit(solution)/shard_map/ppermute | solution.py:381
  73.2 6.7 %collective-permute-start.16 = (f32[256,768]{1,0:T(8,128)S(1)}, f32[256,768]{1,0:T(8,128)S(1)}, u32[]{:S(2)}, u32[]{:S(2)}) collective-permute-start(f32[256,768]{1,0:T(8,128)S(1)} %collective-permute-done.12.refs_2_.refs_4_.refs_0_), channel_id=1, source_target_pairs={{8,12},{12,14},{15,11},{11,7},{7,3},{3,1},{0,4},{4,8},{24,28},{28,... | collective-permute-start | bytes 2359304 | tf_op jit(solution)/shard_map/ppermute | solution.py:381
  79.9 1.3 %collective-permute-start.17 = (f32[256,768]{1,0:T(8,128)S(1)}, f32[256,768]{1,0:T(8,128)S(1)}, u32[]{:S(2)}, u32[]{:S(2)}) collective-permute-start(f32[256,768]{1,0:T(8,128)S(1)} %collective-permute-done.13.refs_1_.refs_6_.refs_4_), channel_id=1, source_target_pairs={{6,10},{2,6},{1,3},{5,1},{9,5},{13,9},{14,12},{10,14},{22,26},{18,... | collective-permute-start | bytes 2359304 | tf_op jit(solution)/shard_map/ppermute | solution.py:381
  81.2 3.4 %tiles.10.refs_5_ = f32[1536,6144]{1,0:T(8,128)} custom-call(bf16[1536,768]{1,0:T(8,128)(2,1)S(1)} %get-tuple-element.30.rows_ref, f32[256,768]{1,0:T(8,128)S(1)} %get-tuple-element.32.refs_2_.refs_0_, f32[256,768]{1,0:T(8,128)S(1)} %collective-permute-done.13.refs_1_.refs_6_.refs_4_, ...), custom_call_target="tpu_custom_call", output_to_operand_aliasing={{}: (5, {})} | custom-call | flops 1811939328 | bytes 4718592 | tf_op jit(solution)/shard_map/tiles/pallas_call | solution.py:291
  84.7 4.5 %collective-permute-start.14 = (f32[256,768]{1,0:T(8,128)S(1)}, f32[256,768]{1,0:T(8,128)S(1)}, u32[]{:S(2)}, u32[]{:S(2)}) collective-permute-start(f32[256,768]{1,0:T(8,128)S(1)} %collective-permute-done.10.refs_2_.refs_5_.refs_1_), channel_id=1, source_target_pairs={{8,12},{12,14},{15,11},{11,7},{7,3},{3,1},{0,4},{4,8},{24,28},{28,... | collective-permute-start | bytes 2359304 | tf_op jit(solution)/shard_map/ppermute | solution.py:381
  89.2 1.3 %collective-permute-start.15 = (f32[256,768]{1,0:T(8,128)S(1)}, f32[256,768]{1,0:T(8,128)S(1)}, u32[]{:S(2)}, u32[]{:S(2)}) collective-permute-start(f32[256,768]{1,0:T(8,128)S(1)} %collective-permute-done.11.refs_1_.refs_7_.refs_5_), channel_id=1, source_target_pairs={{6,10},{2,6},{1,3},{5,1},{9,5},{13,9},{14,12},{10,14},{22,26},{18,... | collective-permute-start | bytes 2359304 | tf_op jit(solution)/shard_map/ppermute | solution.py:381
  90.5 3.6 %tiles.11.refs_8_ = f32[1536,6144]{1,0:T(8,128)} custom-call(bf16[1536,768]{1,0:T(8,128)(2,1)S(1)} %get-tuple-element.30.rows_ref, f32[256,768]{1,0:T(8,128)S(1)} %get-tuple-element.31.refs_1_.refs_3_.refs_0_, f32[256,768]{1,0:T(8,128)S(1)} %collective-permute-done.11.refs_1_.refs_7_.refs_5_, ...), custom_call_target="tpu_custom_call", output_to_operand_aliasing={{}: (6, {})} | custom-call | flops 1811939328 | bytes 4718592 | tf_op jit(solution)/shard_map/tiles/pallas_call | solution.py:291
  94.3 4.2 %collective-permute-done.17.refs_3_.refs_7_ = f32[256,768]{1,0:T(8,128)S(1)} collective-permute-done((f32[256,768]{1,0:T(8,128)S(1)}, f32[256,768]{1,0:T(8,128)S(1)}, u32[]{:S(2)}, u32[]{:S(2)}) %collective-permute-start.17) | collective-permute-done | bytes 786464 | tf_op jit(solution)/shard_map/ppermute | solution.py:381
  98.5 1.9 %collective-permute-start.20 = (f32[128,768]{1,0:T(8,128)S(1)}, f32[128,768]{1,0:T(8,128)S(1)}, u32[]{:S(2)}, u32[]{:S(2)}) collective-permute-start(f32[128,768]{1,0:T(8,128)S(1)} %slice.14), channel_id=1, source_target_pairs={{12,14},{14,10},{11,7},{7,3},{3,1},{1,5},{4,8},{8,12},{28,30},{30,... | collective-permute-start | bytes 1179656 | tf_op jit(solution)/shard_map/ppermute | solution.py:381
  100.4 3.9 %collective-permute-start.21 = (f32[128,768]{1,0:T(8,128)S(1)}, f32[128,768]{1,0:T(8,128)S(1)}, u32[]{:S(2)}, u32[]{:S(2)}) collective-permute-start(f32[128,768]{1,0:T(8,128)S(1)} %slice.15), channel_id=1, source_target_pairs={{10,14},{6,10},{3,7},{1,3},{5,1},{9,5},{12,8},{14,12},{26,30},{22,... | collective-permute-start | bytes 1179656 | tf_op jit(solution)/shard_map/ppermute | solution.py:381
  104.4 5.5 %tiles.12.refs_8_ = f32[1536,6144]{1,0:T(8,128)} custom-call(bf16[1536,768]{1,0:T(8,128)(2,1)S(1)} %get-tuple-element.30.rows_ref, f32[256,768]{1,0:T(8,128)S(1)} %collective-permute-done.6.refs_2_.refs_3_.refs_0_, f32[256,768]{1,0:T(8,128)S(1)} %collective-permute-done.7.refs_1_.refs_4_, ...), custom_call_target="tpu_custom_call", output_to_operand_aliasing={{}: (9, {})} | custom-call | flops 3623878656 | bytes 9437184 | tf_op jit(solution)/shard_map/tiles/pallas_call | solution.py:291
  109.9 1.9 %collective-permute-start.18 = (f32[128,768]{1,0:T(8,128)S(1)}, f32[128,768]{1,0:T(8,128)S(1)}, u32[]{:S(2)}, u32[]{:S(2)}) collective-permute-start(f32[128,768]{1,0:T(8,128)S(1)} %slice.12), channel_id=1, source_target_pairs={{12,14},{14,10},{11,7},{7,3},{3,1},{1,5},{4,8},{8,12},{28,30},{30,... | collective-permute-start | bytes 1179656 | tf_op jit(solution)/shard_map/ppermute | solution.py:381
  111.9 3.9 %collective-permute-start.19 = (f32[128,768]{1,0:T(8,128)S(1)}, f32[128,768]{1,0:T(8,128)S(1)}, u32[]{:S(2)}, u32[]{:S(2)}) collective-permute-start(f32[128,768]{1,0:T(8,128)S(1)} %slice.13), channel_id=1, source_target_pairs={{10,14},{6,10},{3,7},{1,3},{5,1},{9,5},{12,8},{14,12},{26,30},{22,... | collective-permute-start | bytes 1179656 | tf_op jit(solution)/shard_map/ppermute | solution.py:381
  115.8 5.5 %tiles.13.refs_2_ = f32[1536,6144]{1,0:T(8,128)} custom-call(bf16[1536,768]{1,0:T(8,128)(2,1)S(1)} %get-tuple-element.30.rows_ref, f32[256,768]{1,0:T(8,128)S(1)} %collective-permute-done.12.refs_2_.refs_4_.refs_0_, f32[256,768]{1,0:T(8,128)S(1)} %collective-permute-done.10.refs_2_.refs_5_.refs_1_, ...), custom_call_target="tpu_custom_call", output_to_operand_aliasing={{}: (9, {})} | custom-call | flops 3623878656 | bytes 9437184 | tf_op jit(solution)/shard_map/tiles/pallas_call | solution.py:291
  121.4 3.7 %tiles.14.refs_2_ = f32[1536,6144]{1,0:T(8,128)} custom-call(bf16[1536,768]{1,0:T(8,128)(2,1)S(1)} %get-tuple-element.30.rows_ref, f32[128,768]{1,0:T(8,128)S(1)} %collective-permute-done.20.refs_0_, f32[128,768]{1,0:T(8,128)S(1)} %collective-permute-done.21.refs_1_, f32[1536,6144]{1,0:T(8,128)} %tiles.13.refs_2_), custom_call_target="tpu_custom_call", output_to_operand_aliasing={{}: (3, {})} | custom-call | flops 1811939328 | bytes 4718592 | tf_op jit(solution)/shard_map/tiles/pallas_call | solution.py:291
  125.1 3.7 %tiles.15 = f32[1536,6144]{1,0:T(8,128)} custom-call(bf16[1536,768]{1,0:T(8,128)(2,1)S(1)} %get-tuple-element.30.rows_ref, f32[128,768]{1,0:T(8,128)S(1)} %collective-permute-done.18.refs_0_, f32[128,768]{1,0:T(8,128)S(1)} %collective-permute-done.19.refs_1_, f32[1536,6144]{1,0:T(8,128)} %tiles.14.refs_2_), custom_call_target="tpu_custom_call", output_to_operand_aliasing={{}: (3, {})} | custom-call | flops 1811939328 | bytes 4718592 | tf_op jit(solution)/shard_map/tiles/pallas_call | solution.py:291
  (34 shorter events, 5.5 us)
Async XLA Ops:
  0.0 4.1 %collective-permute-start = (f32[1,32,256]{2,1,0:T(8,128)}, f32[1,32,256]{2,1,0:T(8,128)S(1)}, u32[]{:S(2)}, u32[]{:S(2)}) collective-permute-start(f32[1,32,256]{2,1,0:T(8,128)} %bitcast.1), channel_id=1, source_target_pairs={{0,2},{1,3},{2,0},{3,1},{4,6},{5,7},{6,4},{7,5},{8,10},{9,11},{10,... | collective-permute-start | bytes 98312 | tf_op jit(solution)/shard_map/ppermute | solution.py:319
  4.9 4.3 %collective-permute-start.1 = (f32[2,32,256]{2,1,0:T(8,128)S(1)}, f32[2,32,256]{2,1,0:T(8,128)S(1)}, u32[]{:S(2)}, u32[]{:S(2)}) collective-permute-start(f32[2,32,256]{2,1,0:T(8,128)S(1)} %pad_maximum_fusion.1), channel_id=1, source_target_pairs={{0,4},{1,5},{2,6},{3,7},{4,0},{5,1},{6,2},{7,3},{8,12},{9,13},{10,... | collective-permute-start | bytes 196616 | tf_op jit(solution)/shard_map/ppermute | solution.py:319
  5.3 47.8 %collective-permute-start.8 = (f32[768,512]{1,0:T(8,128)}, f32[768,512]{1,0:T(8,128)S(1)}, u32[]{:S(2)}, u32[]{:S(2)}) collective-permute-start(f32[768,512]{1,0:T(8,128)} %refs_0_.1), channel_id=1, source_target_pairs={{0,4},{4,8},{8,13},{12,15},{14,11},{10,7},{6,2},{2,0},{16,20},{20,... | collective-permute-start | bytes 4718600 | tf_op jit(solution)/shard_map/ppermute | solution.py:381
  6.8 46.3 %collective-permute-start.9 = (f32[768,512]{1,0:T(8,128)}, f32[768,512]{1,0:T(8,128)S(1)}, u32[]{:S(2)}, u32[]{:S(2)}) collective-permute-start(f32[768,512]{1,0:T(8,128)} %refs_0_.1), channel_id=1, source_target_pairs={{0,2},{4,0},{8,5},{12,9},{14,13},{10,15},{6,10},{2,6},{16,18},{20,... | collective-permute-start | bytes 4718600 | tf_op jit(solution)/shard_map/ppermute | solution.py:381
  8.2 49.3 %collective-permute-start.5 = (f32[768,512]{1,0:T(8,128)}, f32[768,512]{1,0:T(8,128)S(1)}, u32[]{:S(2)}, u32[]{:S(2)}) collective-permute-start(f32[768,512]{1,0:T(8,128)} %refs_0_.1), channel_id=1, source_target_pairs={{0,1},{1,0},{2,3},{3,2},{4,5},{5,4},{6,7},{7,6},{8,9},{9,8},{10,11... | collective-permute-start | bytes 4718600 | tf_op jit(solution)/shard_map/ppermute | solution.py:410
  9.9 24.6 %collective-permute-start.2 = (f32[4,32,256]{2,1,0:T(8,128)S(1)}, f32[4,32,256]{2,1,0:T(8,128)S(1)}, u32[]{:S(2)}, u32[]{:S(2)}) collective-permute-start(f32[4,32,256]{2,1,0:T(8,128)S(1)} %pad_maximum_fusion.refs_0_), channel_id=1, source_target_pairs={{0,8},{1,9},{2,10},{3,11},{4,12},{5,13},{6,14},{7,15},{8,0},{9,1},... | collective-permute-start | bytes 393224 | tf_op jit(solution)/shard_map/ppermute | solution.py:325
  12.6 21.9 %collective-permute-start.3 = (f32[4,32,256]{2,1,0:T(8,128)S(1)}, f32[4,32,256]{2,1,0:T(8,128)S(1)}, u32[]{:S(2)}, u32[]{:S(2)}) collective-permute-start(f32[4,32,256]{2,1,0:T(8,128)S(1)} %pad_maximum_fusion.refs_0_), channel_id=1, source_target_pairs={{0,1},{1,0},{2,3},{3,2},{4,5},{5,4},{6,7},{7,6},{8,9},{9,8},{10,11... | collective-permute-start | bytes 393224 | tf_op jit(solution)/shard_map/ppermute | solution.py:325
  34.5 1.3 %collective-permute-start.4 = (f32[4,32,256]{2,1,0:T(8,128)S(1)}, f32[4,32,256]{2,1,0:T(8,128)S(1)}, u32[]{:S(2)}, u32[]{:S(2)}) collective-permute-start(f32[4,32,256]{2,1,0:T(8,128)S(1)} %collective-permute-done.2.refs_1_), channel_id=1, source_target_pairs={{0,1},{1,0},{2,3},{3,2},{4,5},{5,4},{6,7},{7,6},{8,9},{9,8},{10,11... | collective-permute-start | bytes 393224 | tf_op jit(solution)/shard_map/ppermute | solution.py:325
  49.3 1.4 %copy-start = (f32[768,512]{1,0:T(8,128)S(1)}, f32[768,512]{1,0:T(8,128)}, u32[]{:S(2)}) copy-start(f32[768,512]{1,0:T(8,128)} %refs_0_.1) | copy-start | bytes 4718596
  51.7 10.0 %collective-permute-start.6 = (f32[256,768]{1,0:T(8,128)S(1)}, f32[256,768]{1,0:T(8,128)S(1)}, u32[]{:S(2)}, u32[]{:S(2)}) collective-permute-start(f32[256,768]{1,0:T(8,128)S(1)} %project.2.refs_0_), channel_id=1, source_target_pairs={{1,4},{5,8},{9,13},{13,15},{15,11},{11,7},{7,2},{3,0},{17,20},{21,... | collective-permute-start | bytes 2359304 | tf_op jit(solution)/shard_map/ppermute | solution.py:381
  52.4 9.3 %collective-permute-start.7 = (f32[256,768]{1,0:T(8,128)S(1)}, f32[256,768]{1,0:T(8,128)S(1)}, u32[]{:S(2)}, u32[]{:S(2)}) collective-permute-start(f32[256,768]{1,0:T(8,128)S(1)} %project.2.refs_0_), channel_id=1, source_target_pairs={{1,2},{5,0},{9,5},{13,9},{15,13},{11,15},{7,10},{3,6},{17,18},{21,... | collective-permute-start | bytes 2359304 | tf_op jit(solution)/shard_map/ppermute | solution.py:381
  55.6 8.3 %collective-permute-start.13 = (f32[256,768]{1,0:T(8,128)S(1)}, f32[256,768]{1,0:T(8,128)S(1)}, u32[]{:S(2)}, u32[]{:S(2)}) collective-permute-start(f32[256,768]{1,0:T(8,128)S(1)} %get-tuple-element.31.refs_1_.refs_3_.refs_0_), channel_id=1, source_target_pairs={{2,6},{0,2},{5,1},{9,5},{13,9},{15,13},{10,14},{6,10},{18,22},{16,... | collective-permute-start | bytes 2359304 | tf_op jit(solution)/shard_map/ppermute | solution.py:381
  56.3 16.9 %collective-permute-start.12 = (f32[256,768]{1,0:T(8,128)S(1)}, f32[256,768]{1,0:T(8,128)S(1)}, u32[]{:S(2)}, u32[]{:S(2)}) collective-permute-start(f32[256,768]{1,0:T(8,128)S(1)} %get-tuple-element.32.refs_2_.refs_0_), channel_id=1, source_target_pairs={{4,8},{8,12},{13,15},{15,11},{11,7},{7,3},{2,0},{0,4},{20,24},{24,... | collective-permute-start | bytes 2359304 | tf_op jit(solution)/shard_map/ppermute | solution.py:381
  57.6 1.4 %copy-start.1 = (f32[768,512]{1,0:T(8,128)S(1)}, f32[768,512]{1,0:T(8,128)}, u32[]{:S(2)}) copy-start(f32[768,512]{1,0:T(8,128)} %refs_0_.1) | copy-start | bytes 4718596
  61.7 22.9 %collective-permute-start.10 = (f32[256,768]{1,0:T(8,128)S(1)}, f32[256,768]{1,0:T(8,128)S(1)}, u32[]{:S(2)}, u32[]{:S(2)}) collective-permute-start(f32[256,768]{1,0:T(8,128)S(1)} %collective-permute-done.6.refs_2_.refs_3_.refs_0_), channel_id=1, source_target_pairs={{4,8},{8,12},{13,15},{15,11},{11,7},{7,3},{2,0},{0,4},{20,24},{24,... | collective-permute-start | bytes 2359304 | tf_op jit(solution)/shard_map/ppermute | solution.py:381
  63.0 21.6 %collective-permute-start.11 = (f32[256,768]{1,0:T(8,128)S(1)}, f32[256,768]{1,0:T(8,128)S(1)}, u32[]{:S(2)}, u32[]{:S(2)}) collective-permute-start(f32[256,768]{1,0:T(8,128)S(1)} %collective-permute-done.7.refs_1_.refs_4_), channel_id=1, source_target_pairs={{2,6},{0,2},{5,1},{9,5},{13,9},{15,13},{10,14},{6,10},{18,22},{16,... | collective-permute-start | bytes 2359304 | tf_op jit(solution)/shard_map/ppermute | solution.py:381
  73.2 21.0 %collective-permute-start.16 = (f32[256,768]{1,0:T(8,128)S(1)}, f32[256,768]{1,0:T(8,128)S(1)}, u32[]{:S(2)}, u32[]{:S(2)}) collective-permute-start(f32[256,768]{1,0:T(8,128)S(1)} %collective-permute-done.12.refs_2_.refs_4_.refs_0_), channel_id=1, source_target_pairs={{8,12},{12,14},{15,11},{11,7},{7,3},{3,1},{0,4},{4,8},{24,28},{28,... | collective-permute-start | bytes 2359304 | tf_op jit(solution)/shard_map/ppermute | solution.py:381
  79.9 18.5 %collective-permute-start.17 = (f32[256,768]{1,0:T(8,128)S(1)}, f32[256,768]{1,0:T(8,128)S(1)}, u32[]{:S(2)}, u32[]{:S(2)}) collective-permute-start(f32[256,768]{1,0:T(8,128)S(1)} %collective-permute-done.13.refs_1_.refs_6_.refs_4_), channel_id=1, source_target_pairs={{6,10},{2,6},{1,3},{5,1},{9,5},{13,9},{14,12},{10,14},{22,26},{18,... | collective-permute-start | bytes 2359304 | tf_op jit(solution)/shard_map/ppermute | solution.py:381
  84.7 25.2 %collective-permute-start.14 = (f32[256,768]{1,0:T(8,128)S(1)}, f32[256,768]{1,0:T(8,128)S(1)}, u32[]{:S(2)}, u32[]{:S(2)}) collective-permute-start(f32[256,768]{1,0:T(8,128)S(1)} %collective-permute-done.10.refs_2_.refs_5_.refs_1_), channel_id=1, source_target_pairs={{8,12},{12,14},{15,11},{11,7},{7,3},{3,1},{0,4},{4,8},{24,28},{28,... | collective-permute-start | bytes 2359304 | tf_op jit(solution)/shard_map/ppermute | solution.py:381
  89.2 20.7 %collective-permute-start.15 = (f32[256,768]{1,0:T(8,128)S(1)}, f32[256,768]{1,0:T(8,128)S(1)}, u32[]{:S(2)}, u32[]{:S(2)}) collective-permute-start(f32[256,768]{1,0:T(8,128)S(1)} %collective-permute-done.11.refs_1_.refs_7_.refs_5_), channel_id=1, source_target_pairs={{6,10},{2,6},{1,3},{5,1},{9,5},{13,9},{14,12},{10,14},{22,26},{18,... | collective-permute-start | bytes 2359304 | tf_op jit(solution)/shard_map/ppermute | solution.py:381
  98.5 22.9 %collective-permute-start.20 = (f32[128,768]{1,0:T(8,128)S(1)}, f32[128,768]{1,0:T(8,128)S(1)}, u32[]{:S(2)}, u32[]{:S(2)}) collective-permute-start(f32[128,768]{1,0:T(8,128)S(1)} %slice.14), channel_id=1, source_target_pairs={{12,14},{14,10},{11,7},{7,3},{3,1},{1,5},{4,8},{8,12},{28,30},{30,... | collective-permute-start | bytes 1179656 | tf_op jit(solution)/shard_map/ppermute | solution.py:381
  100.4 21.0 %collective-permute-start.21 = (f32[128,768]{1,0:T(8,128)S(1)}, f32[128,768]{1,0:T(8,128)S(1)}, u32[]{:S(2)}, u32[]{:S(2)}) collective-permute-start(f32[128,768]{1,0:T(8,128)S(1)} %slice.15), channel_id=1, source_target_pairs={{10,14},{6,10},{3,7},{1,3},{5,1},{9,5},{12,8},{14,12},{26,30},{22,... | collective-permute-start | bytes 1179656 | tf_op jit(solution)/shard_map/ppermute | solution.py:381
  109.9 15.2 %collective-permute-start.18 = (f32[128,768]{1,0:T(8,128)S(1)}, f32[128,768]{1,0:T(8,128)S(1)}, u32[]{:S(2)}, u32[]{:S(2)}) collective-permute-start(f32[128,768]{1,0:T(8,128)S(1)} %slice.12), channel_id=1, source_target_pairs={{12,14},{14,10},{11,7},{7,3},{3,1},{1,5},{4,8},{8,12},{28,30},{30,... | collective-permute-start | bytes 1179656 | tf_op jit(solution)/shard_map/ppermute | solution.py:381
  111.9 13.2 %collective-permute-start.19 = (f32[128,768]{1,0:T(8,128)S(1)}, f32[128,768]{1,0:T(8,128)S(1)}, u32[]{:S(2)}, u32[]{:S(2)}) collective-permute-start(f32[128,768]{1,0:T(8,128)S(1)} %slice.13), channel_id=1, source_target_pairs={{10,14},{6,10},{3,7},{1,3},{5,1},{9,5},{12,8},{14,12},{26,30},{22,... | collective-permute-start | bytes 1179656 | tf_op jit(solution)/shard_map/ppermute | solution.py:381
where the time goes:
time: 130 us; the launch traced here: 129 us
  Pallas kernels  45 us (35%)
  waiting for transfers between devices  40.2 us (31%)
  starting transfers between devices  38.8 us (30%)
  local copies, waits for them, and re-layouts  2.91 us (2%)
  other arithmetic  1.53 us (1%)
    ppermute x16, starting transfers between devices, hop(): return lax.ppermute(x, AXES, pairs)  33.9 us
    pallas_call x8, Pallas kernels, tiles(): pl.pallas_call(functools.partial(tiles_kernel, [len(piece) for piece in p...  25.6 us
    ppermute x3, waiting for transfers between devices, gather_all(): lax.ppermute(source, AXES, [(i, i ^ (1 if flip & 1 else flip)) for i in r...  23 us
    ppermute x16, waiting for transfers between devices, hop(): return lax.ppermute(x, AXES, pairs)  13.7 us
    pallas_call x1, Pallas kernels, basis(): pl.pallas_call(functools.partial(basis_kernel, len(parts), spots), out_sh...  13.4 us
    ppermute x2, waiting for transfers between devices, gather_all(): other = lax.ppermute(y, AXES, [(i, i ^ bit) for i in range(n)])  3.47 us
    pallas_call x2, Pallas kernels, project(): pl.pallas_call(functools.partial(project_kernel, count), out_shape=[jax.S...  3.41 us
    ppermute x3, starting transfers between devices, gather_all(): lax.ppermute(source, AXES, [(i, i ^ (1 if flip & 1 else flip)) for i in r...  2.9 us
  transfers between devices with their start and end apart: 22, of which 7 were waited for; matrix products, arithmetic and copies ran while one was open for 1% of the time, Pallas kernels for 32%

commit v1 on v0

--- a/solution.py
+++ b/solution.py
@@ -14,7 +14,6 @@
 NN = (((1,), (0,)), ((), ()))
 TN = (((0,), (0,)), ((), ()))
 NT = (((1,), (1,)), ((), ()))
-TT = (((0,), (1,)), ((), ()))
 
 
 def low(a, b, dims=NN):
@@ -43,9 +42,12 @@
     return jnp.where(r == c, 1.0, 0.0).astype(f32)
 
 
-def basis_kernel(count, spots, *refs):
-    parts, (c_ref, x_ref, g_ref, v_ref, b_ref, z_ref, s_ref, e_ref) = refs[:count], refs[count:]
+def basis_kernel(count, spots, slab_ref, *refs):
+    parts, refs = refs[:count], refs[count:]
+    c_ref, w_ref, x_ref, g_ref, v_ref, b_ref, z_ref, s_ref, e_ref, held, sem = refs
     m, n = x_ref.shape
+    load = pltpu.make_async_copy(slab_ref, held, sem)
+    load.start()
     blocks, size = parts[0].shape[:2]
     for i, part in enumerate(parts):
         for j in range(blocks):
@@ -68,27 +70,35 @@
         v = v + low(v, 0.5 * k + 0.375 * low(k, k))
     v_ref[...] = v
 
-    def polish(dot=high):
+    def polish(k):
+        v = v_ref[...]
+        k2 = low(k, k)
+        v_ref[...] = v + mid(v, 0.5 * k + 0.375 * k2 + 0.3125 * low(k, k2))
+
+    def off(dot=high):
         v = v_ref[...]
         k = ident - dot(v, dot(g_ref[...], v), TN)
-        k2 = low(k, k)
-        v_ref[...] = v + mid(v, 0.5 * k + 0.375 * k2 + 0.3125 * low(k, k2))
+        e_ref[...] = k
         return jnp.max(jnp.abs(k))
 
-    polish(mid)
+    def again(at):
+        polish(e_ref[...])
+        return at[0] + 1, off()
+
+    off(mid)
+    polish(e_ref[...])
     lax.while_loop(
-        lambda at: jnp.logical_and(at[0] < 60, jnp.logical_not(at[1] < 1e-4)),
-        lambda at: (at[0] + 1, polish()),
-        (jnp.int32(0), polish()),
+        lambda at: jnp.logical_and(at[0] < 60, jnp.logical_not(at[1] < 1e-4)), again, (jnp.int32(0), off())
     )
-    v = v_ref[...] * lax.rsqrt(bound)
+    v = v_ref[...]
+    v = (v + low(v, 0.5 * e_ref[...])) * lax.rsqrt(bound)
     v_ref[...] = v
     q1 = high(x, v)
     a = q1[:n]
     s = jnp.where(jnp.sum(a * ident, axis=0, keepdims=True) < 0, 1.0, -1.0).astype(f32)
     s_ref[...] = s
-    p = low(v, x[:n], TT) * s
-    b_ref[...] = ident - high(v, x[:n], TT) * s
+    p = a.T * s
+    b_ref[...] = ident - a.T * s
     z = ident + p
     for _ in range(4):
         p = low(p, p)
@@ -106,7 +116,7 @@
 
     @pl.when(jnp.logical_not(error < 3e-5))
     def _():
-        e_ref[...] = high(x_ref[:n], v_ref[...])
+        e_ref[...] = q1[:n]
         rows = lax.broadcasted_iota(jnp.int32, (n, n), 0)
         cols = lax.broadcasted_iota(jnp.int32, (n, n), 1)
         lane = lax.broadcasted_iota(jnp.int32, (1, n), 1)
@@ -123,7 +133,7 @@
 
         s = lax.fori_loop(0, n, step, jnp.zeros((1, n), f32))
         s_ref[...] = s
-        b = eye(n) - high(v_ref[...], x_ref[:n], TT) * s
+        b = eye(n) - q1[:n].T * s
         b_ref[...] = b
         z_ref[...] = 0.49 * b.T
         lax.while_loop(
@@ -137,23 +147,27 @@
     nt = -high(q2, z_ref[...], NT)
     c_ref[:, :n] = high(nt, a - ident * s_ref[...], NT)
     c_ref[:, n:] = eye(m - n) + high(nt, q2, NT)
-
-
-def basis(parts, spots):
+    load.wait()
+    ch, cl = halves(c_ref[...])
+    h, l = halves(held[...])
+    w_ref[...] = lax.dot_general(beside(ch, cl, ch), beside(h, h, l), NT, preferred_element_type=f32)
+
+
+def basis(slab, parts, spots):
     blocks, size, n = parts[0].shape
     m = len(parts) * blocks * size
     return pl.pallas_call(
         functools.partial(basis_kernel, len(parts), spots),
-        out_shape=jax.ShapeDtypeStruct((m - n, m), f32),
-        in_specs=[pl.BlockSpec(memory_space=pltpu.VMEM)] * len(parts),
-        out_specs=pl.BlockSpec(memory_space=pltpu.VMEM),
+        out_shape=[jax.ShapeDtypeStruct((m - n, m), f32), jax.ShapeDtypeStruct((m - n, slab.shape[0]), f32)],
+        in_specs=[pl.BlockSpec(memory_space=pl.ANY)] + [pl.BlockSpec(memory_space=pltpu.VMEM)] * len(parts),
+        out_specs=[pl.BlockSpec(memory_space=pltpu.VMEM)] * 2,
         scratch_shapes=[pltpu.VMEM((m, n), f32)]
         + [pltpu.VMEM((n, n), f32)] * 4
-        + [pltpu.VMEM((1, n), f32), pltpu.VMEM((n, n), f32)],
+        + [pltpu.VMEM((1, n), f32), pltpu.VMEM((n, n), f32), pltpu.VMEM(slab.shape, f32), pltpu.SemaphoreType.DMA],
         compiler_params=pltpu.CompilerParams(vmem_limit_bytes=24 << 20),
         cost_estimate=pl.CostEstimate(flops=8_000_000_000, bytes_accessed=1 << 20, transcendentals=0),
         name="basis",
-    )(*parts)
+    )(slab, *parts)
 
 
 def pick(column):
@@ -199,36 +213,30 @@
     )(comp, *pieces)
 
 
-def own_kernel(c_ref, mine_ref, theirs_ref, rows_ref, b_ref, held, sem):
+def own_kernel(samples, c_ref, mine_ref, theirs_ref, rows_ref, b_ref):
     core = lax.axis_index("col")
-    shard, samples = held.shape[1:]
-    for i, ref in enumerate((mine_ref, theirs_ref)):
-        pltpu.make_async_copy(ref, held.at[i], sem.at[i]).start()
+    shard = mine_ref.shape[1]
     ch, cl = halves(c_ref[...])
-    left, right = beside(ch, cl, ch), beside(ch, ch, cl)
-    for i, ref in enumerate((mine_ref, theirs_ref)):
-        pltpu.make_async_copy(ref, held.at[i], sem.at[i]).wait()
-        h, l = halves(held[i])
-        if i == 1:
-            b_ref[...] = lax.dot_general(left, beside(h, h, l), NT, preferred_element_type=f32)
-        w = lax.dot_general(beside(h, l, h), right, NT, preferred_element_type=f32) * (1.0 / samples)
-        h, l = halves(w)
+    h, l = halves(theirs_ref[...])
+    theirs = lax.dot_general(beside(ch, cl, ch), beside(h, h, l), NT, preferred_element_type=f32)
+    b_ref[...] = theirs
+    for i, w in enumerate((mine_ref[...], theirs)):
+        h, l = halves(w.T * (1.0 / samples))
         at = pl.ds(pl.multiple_of((core if i == 0 else 1 - core) * shard, shard), shard)
         rows_ref[at, :] = beside(h, l, h)
 
 
 def own_parts(comp, mine, theirs):
-    shard, samples = mine.shape
+    shard, samples = theirs.shape
     k = comp.shape[0]
     return pl.pallas_call(
-        own_kernel,
+        functools.partial(own_kernel, samples),
         out_shape=[jax.ShapeDtypeStruct((2 * shard, 3 * k), bf16), jax.ShapeDtypeStruct((k, shard), f32)],
-        in_specs=[pl.BlockSpec(memory_space=pltpu.VMEM)] + [pl.BlockSpec(memory_space=pltpu.HBM)] * 2,
+        in_specs=[pl.BlockSpec(memory_space=pltpu.VMEM)] * 3,
         out_specs=[pl.BlockSpec(memory_space=pltpu.VMEM)] * 2,
-        scratch_shapes=[pltpu.VMEM((2, shard, samples), f32), pltpu.SemaphoreType.DMA((2,))],
         compiler_params=pltpu.CompilerParams(vmem_limit_bytes=24 << 20),
         cost_estimate=pl.CostEstimate(
-            flops=18 * shard * samples * k, bytes_accessed=8 * shard * (samples + 2 * k), transcendentals=0
+            flops=6 * shard * samples * k, bytes_accessed=8 * shard * (samples + 2 * k), transcendentals=0
         ),
         name="own",
     )(comp, mine, theirs)
@@ -314,16 +322,16 @@
     if n & (n - 1) or n_col != 2 or n < 8 or x.shape[0] % 8:
         return [lax.all_gather(x, AXES, axis=0, tiled=True)[None]], np.zeros((n, 1), np.int32)
     y, held = x[None], [0]
-    bit = n_col
-    while 2 * bit < n:
+    bit = n // 2
+    while bit > n_col:
         other = lax.ppermute(y, AXES, [(i, i ^ bit) for i in range(n)])
         y, held = jnp.concatenate([y, other]), held + [h ^ bit for h in held]
-        bit *= 2
-    parts, spots = [y], list(held)
-    for flip in (bit, 1, bit + 1):
-        source = parts[1] if flip == bit + 1 else y
-        parts.append(lax.ppermute(source, AXES, [(i, i ^ (1 if flip & 1 else flip)) for i in range(n)]))
-        spots += [h ^ flip for h in held]
+        bit //= 2
+    far = lax.ppermute(y, AXES, [(i, i ^ bit) for i in range(n)])
+    core = [(i, i ^ 1) for i in range(n)]
+    parts = [y, far, lax.ppermute(y, AXES, core)]
+    parts.append(lax.ppermute(far, AXES, core))
+    spots = [h ^ flip for flip in (0, bit, 1, bit + 1) for h in held]
     return parts, np.array([[i ^ h for h in spots] for i in range(n)], np.int32)
 
 
@@ -362,7 +370,7 @@
     width = n_row * shard
 
     if n_col != 2 or n_row % 2 or shard % 128:
-        comp = basis(*gather_all(predictors, n_row, n_col))
+        comp, _ = basis(slab, *gather_all(predictors, n_row, n_col))
         w = lax.dot_general(slab, comp, NT, precision=lax.Precision.HIGHEST)
         every = lax.all_gather(w, AXES, axis=0, tiled=True)
         cols = lax.dynamic_slice_in_dim(every, lax.axis_index("col") * width, width)
@@ -406,10 +414,11 @@
         return tiles(table, rows, [todo[1][key] for key in names], out, width)
 
     half = n_row // 2
-    near = {way: hop(slab, way, 1, 0) for way in (1, -1)}
+    near = {}
+    for way in (1, -1):
+        near[way] = hop(slab, way, 1, 0)
     other = lax.ppermute(slab, "col", [(0, 1), (1, 0)])
-    comp = basis(*gather_all(predictors, n_row, n_col))
-    (mine,) = project(comp, [slab])
+    comp, mine = basis(slab, *gather_all(predictors, n_row, n_col))
     flights = [(1, 1, {way: hop(mine, way, 1, 1) for way in (1, -1)})]
     first = dict(zip((1, -1), project(comp, [near[1], near[-1]])))
 
@@ -421,7 +430,7 @@
             flights.append((core, half, {1: hop(sent[1][:k], 1, half), -1: hop(sent[-1][k:], -1, half)}))
 
     onward(0, 1, first)
-    rows, theirs = own_parts(comp, slab, other)
+    rows, theirs = own_parts(comp, mine, other)
     arrive(0, "mine", [mine])
     arrive(0, "theirs", [theirs])
     for way in (1, -1):
@@ -429,6 +438,9 @@
     out = work(rows, None, 1)
     while flights:
         core, steps, sent = flights.pop(0)
+        if steps == half and flights:
+            core, steps, sent = core, half, {(c, way): w for c, _, ws in [(core, half, sent)] + flights for way, w in ws.items()}
+            flights.clear()
         got = lax.optimization_barrier(tuple(sent.values()) + (out,))
         out = got[-1]
         sent = dict(zip(sent, got))
@@ -437,7 +449,8 @@
             for way, w in sent.items():
                 arrive(-way * steps, core, [w])
         else:
-            arrive(half, core, list(sent.values()))
+            for c in range(n_col):
+                arrive(half, c, [sent[c, 1], sent[c, -1]])
         out = work(rows, out, (1 if steps + 1 < half else 2) if flights else 8)
     return out
 

time: 130 us -> 130 us (level)
  the two profiles are of different devices: /device:TPU:28 before, /device:TPU:20 now
where the time goes in v1:
time: 130 us; the launch traced here: 129 us
  starting transfers between devices  45.1 us (35%)
  Pallas kernels  44.7 us (34%)
  waiting for transfers between devices  36 us (28%)
  other arithmetic  1.53 us (1%)
  local copies, waits for them, and re-layouts  1.52 us (1%)
    ppermute x16, starting transfers between devices, hop(): return lax.ppermute(x, AXES, pairs)  41.9 us
    pallas_call x7, Pallas kernels, tiles(): pl.pallas_call(functools.partial(tiles_kernel, [len(piece) for piece in p...  26.8 us
    ppermute x2, waiting for transfers between devices, gather_all(): other = lax.ppermute(y, AXES, [(i, i ^ bit) for i in range(n)])  17.9 us
    pallas_call x1, Pallas kernels, basis(): pl.pallas_call(functools.partial(basis_kernel, len(parts), spots), out_sh...  14.6 us
    ppermute x16, waiting for transfers between devices, hop(): return lax.ppermute(x, AXES, pairs)  12.9 us
    ppermute x1, waiting for transfers between devices, gather_all(): far = lax.ppermute(y, AXES, [(i, i ^ bit) for i in range(n)])  3.91 us
  transfers between devices with their start and end apart: 22, of which 10 were waited for; matrix products, arithmetic and copies ran while one was open for 1% of the time, Pallas kernels for 30%

profile of v1, /device:TPU:20, one launch (start us, length us, event | category | flops | bytes accessed | tf_op | source)
XLA Modules:
  0.0 129.4 jit_solution(4838908930132195796)
XLA Ops:
  0.3 2.6 %collective-permute-start.6 = (f32[768,512]{1,0:T(8,128)}, f32[768,512]{1,0:T(8,128)S(1)}, u32[]{:S(2)}, u32[]{:S(2)}) collective-permute-start(f32[768,512]{1,0:T(8,128)} %slab_ref.1), channel_id=1, source_target_pairs={{0,4},{4,8},{8,13},{12,15},{14,11},{10,7},{6,2},{2,0},{16,20},{20,... | collective-permute-start | bytes 4718600 | tf_op jit(solution)/shard_map/ppermute | solution.py:389
  3.0 2.0 %collective-permute-start.7 = (f32[768,512]{1,0:T(8,128)}, f32[768,512]{1,0:T(8,128)S(1)}, u32[]{:S(2)}, u32[]{:S(2)}) collective-permute-start(f32[768,512]{1,0:T(8,128)} %slab_ref.1), channel_id=1, source_target_pairs={{0,2},{4,0},{8,5},{12,9},{14,13},{10,15},{6,10},{2,6},{16,18},{20,... | collective-permute-start | bytes 4718600 | tf_op jit(solution)/shard_map/ppermute | solution.py:389
  5.8 1.8 %collective-permute-start.1 = (f32[2,32,256]{2,1,0:T(8,128)S(1)}, f32[2,32,256]{2,1,0:T(8,128)S(1)}, u32[]{:S(2)}, u32[]{:S(2)}) collective-permute-start(f32[2,32,256]{2,1,0:T(8,128)S(1)} %pad_maximum_fusion.1), channel_id=1, source_target_pairs={{0,4},{1,5},{2,6},{3,7},{4,0},{5,1},{6,2},{7,3},{8,12},{9,13},{10,... | collective-permute-start | bytes 196616 | tf_op jit(solution)/shard_map/ppermute | solution.py:327
  7.6 17.8 %collective-permute-done.1 = f32[2,32,256]{2,1,0:T(8,128)S(1)} collective-permute-done((f32[2,32,256]{2,1,0:T(8,128)S(1)}, f32[2,32,256]{2,1,0:T(8,128)S(1)}, u32[]{:S(2)}, u32[]{:S(2)}) %collective-permute-start.1) | collective-permute-done | bytes 65568 | tf_op jit(solution)/shard_map/ppermute | solution.py:327
  25.4 0.8 pad_maximum_fusion.refs_0_
  26.2 1.1 collective-permute-start.2
  27.3 3.9 %collective-permute-done.2.refs_1_ = f32[4,32,256]{2,1,0:T(8,128)S(1)} collective-permute-done((f32[4,32,256]{2,1,0:T(8,128)S(1)}, f32[4,32,256]{2,1,0:T(8,128)S(1)}, u32[]{:S(2)}, u32[]{:S(2)}) %collective-permute-start.2) | collective-permute-done | bytes 131104 | tf_op jit(solution)/shard_map/ppermute | solution.py:330
  31.2 1.3 %collective-permute-done.4.refs_3_ = f32[4,32,256]{2,1,0:T(8,128)S(1)} collective-permute-done((f32[4,32,256]{2,1,0:T(8,128)S(1)}, f32[4,32,256]{2,1,0:T(8,128)S(1)}, u32[]{:S(2)}, u32[]{:S(2)}) %collective-permute-start.4) | collective-permute-done | bytes 131104 | tf_op jit(solution)/shard_map/ppermute | solution.py:333
  32.6 1.4 %copy-done = f32[768,512]{1,0:T(8,128)S(1)} copy-done((f32[768,512]{1,0:T(8,128)S(1)}, f32[768,512]{1,0:T(8,128)}, u32[]{:S(2)}) %copy-start) | copy-done | bytes 1572888
  34.0 14.6 %basis.1 = (f32[256,512]{1,0:T(8,128)S(1)}, f32[256,768]{1,0:T(8,128)S(1)}) custom-call(f32[768,512]{1,0:T(8,128)S(1)} %copy-done, f32[4,32,256]{2,1,0:T(8,128)S(1)} %pad_maximum_fusion.refs_0_, f32[4,32,256]{2,1,0:T(8,128)S(1)} %collective-permute-done.2.refs_1_, f32[4,32,256]{2,1,0:T(8,128)S(1)} %collective-permute-done.3.refs_2_, ...), custom_call_target="tpu_custom_call" | custom-call | flops 8000000000 | bytes 1048576 | tf_op jit(solution)/shard_map/basis/pallas_call | solution.py:159
  48.6 1.3 collective-permute-start.10
  50.6 2.4 %project.1 = (f32[256,768]{1,0:T(8,128)S(1)}, f32[256,768]{1,0:T(8,128)S(1)}) custom-call(f32[256,512]{1,0:T(8,128)S(1)} %get-tuple-element.31.c_ref, f32[768,512]{1,0:T(8,128)S(1)} %collective-permute-done.6.refs_0_, f32[768,512]{1,0:T(8,128)S(1)} %collective-permute-done.7.refs_1_), custom_call_target="tpu_custom_call" | custom-call | flops 1207959552 | bytes 4718592 | tf_op jit(solution)/shard_map/project/pallas_call | solution.py:202
  53.7 2.8 %collective-permute-start.8 = (f32[256,768]{1,0:T(8,128)S(1)}, f32[256,768]{1,0:T(8,128)S(1)}, u32[]{:S(2)}, u32[]{:S(2)}) collective-permute-start(f32[256,768]{1,0:T(8,128)S(1)} %get-tuple-element.34.refs_2_.refs_0_), channel_id=1, source_target_pairs={{4,8},{8,12},{13,15},{15,11},{11,7},{7,3},{2,0},{0,4},{20,24},{24,... | collective-permute-start | bytes 2359304 | tf_op jit(solution)/shard_map/ppermute | solution.py:389
  56.6 1.0 own.1
  57.6 3.4 %tiles.7.refs_3_ = f32[1536,6144]{1,0:T(8,128)} custom-call(bf16[1536,768]{1,0:T(8,128)(2,1)S(1)} %get-tuple-element.33.rows_ref, f32[256,768]{1,0:T(8,128)S(1)} %get-tuple-element.32.mine_ref.refs_0_, f32[256,768]{1,0:T(8,128)S(1)} %get-tuple-element.35.refs_1_.refs_3_.refs_0_, f32[256,768]{1,0:T(8,128)S(1)} %get-tuple-element.34.refs_2_.refs_0_), custom_call_target="tpu_custom_call" | custom-call | flops 1811939328 | bytes 4718592 | tf_op jit(solution)/shard_map/tiles/pallas_call | solution.py:299
  60.9 3.2 %collective-permute-done.10.refs_2_.refs_3_.refs_0_ = f32[256,768]{1,0:T(8,128)S(1)} collective-permute-done((f32[256,768]{1,0:T(8,128)S(1)}, f32[256,768]{1,0:T(8,128)S(1)}, u32[]{:S(2)}, u32[]{:S(2)}) %collective-permute-start.10) | collective-permute-done | bytes 786464 | tf_op jit(solution)/shard_map/ppermute | solution.py:389
  64.2 1.9 %collective-permute-start.14 = (f32[256,768]{1,0:T(8,128)S(1)}, f32[256,768]{1,0:T(8,128)S(1)}, u32[]{:S(2)}, u32[]{:S(2)}) collective-permute-start(f32[256,768]{1,0:T(8,128)S(1)} %collective-permute-done.10.refs_2_.refs_3_.refs_0_), channel_id=1, source_target_pairs={{4,8},{8,12},{13,15},{15,11},{11,7},{7,3},{2,0},{0,4},{20,24},{24,... | collective-permute-start | bytes 2359304 | tf_op jit(solution)/shard_map/ppermute | solution.py:389
  66.8 3.4 %tiles.8.refs_4_ = f32[1536,6144]{1,0:T(8,128)} custom-call(bf16[1536,768]{1,0:T(8,128)(2,1)S(1)} %get-tuple-element.33.rows_ref, f32[256,768]{1,0:T(8,128)S(1)} %get-tuple-element.36.refs_0_, f32[256,768]{1,0:T(8,128)S(1)} %collective-permute-done.11.refs_1_.refs_4_, ...), custom_call_target="tpu_custom_call", output_to_operand_aliasing={{}: (4, {})} | custom-call | flops 1811939328 | bytes 4718592 | tf_op jit(solution)/shard_map/tiles/pallas_call | solution.py:299
  70.5 3.0 %collective-permute-start.12 = (f32[256,768]{1,0:T(8,128)S(1)}, f32[256,768]{1,0:T(8,128)S(1)}, u32[]{:S(2)}, u32[]{:S(2)}) collective-permute-start(f32[256,768]{1,0:T(8,128)S(1)} %collective-permute-done.8.refs_2_.refs_4_.refs_0_), channel_id=1, source_target_pairs={{8,12},{12,14},{15,11},{11,7},{7,3},{3,1},{0,4},{4,8},{24,28},{28,... | collective-permute-start | bytes 2359304 | tf_op jit(solution)/shard_map/ppermute | solution.py:389
  74.2 3.4 %tiles.9.refs_5_ = f32[1536,6144]{1,0:T(8,128)} custom-call(bf16[1536,768]{1,0:T(8,128)(2,1)S(1)} %get-tuple-element.33.rows_ref, f32[256,768]{1,0:T(8,128)S(1)} %get-tuple-element.34.refs_2_.refs_0_, f32[256,768]{1,0:T(8,128)S(1)} %collective-permute-done.9.refs_1_.refs_6_.refs_4_, ...), custom_call_target="tpu_custom_call", output_to_operand_aliasing={{}: (5, {})} | custom-call | flops 1811939328 | bytes 4718592 | tf_op jit(solution)/shard_map/tiles/pallas_call | solution.py:299
  77.6 1.3 %collective-permute-done.14.refs_2_.refs_5_.refs_1_ = f32[256,768]{1,0:T(8,128)S(1)} collective-permute-done((f32[256,768]{1,0:T(8,128)S(1)}, f32[256,768]{1,0:T(8,128)S(1)}, u32[]{:S(2)}, u32[]{:S(2)}) %collective-permute-start.14) | collective-permute-done | bytes 786464 | tf_op jit(solution)/shard_map/ppermute | solution.py:389
  78.9 5.8 %collective-permute-start.18 = (f32[256,768]{1,0:T(8,128)S(1)}, f32[256,768]{1,0:T(8,128)S(1)}, u32[]{:S(2)}, u32[]{:S(2)}) collective-permute-start(f32[256,768]{1,0:T(8,128)S(1)} %collective-permute-done.14.refs_2_.refs_5_.refs_1_), channel_id=1, source_target_pairs={{8,12},{12,14},{15,11},{11,7},{7,3},{3,1},{0,4},{4,8},{24,28},{28,... | collective-permute-start | bytes 2359304 | tf_op jit(solution)/shard_map/ppermute | solution.py:389
  85.4 3.4 %tiles.10.refs_8_ = f32[1536,6144]{1,0:T(8,128)} custom-call(bf16[1536,768]{1,0:T(8,128)(2,1)S(1)} %get-tuple-element.33.rows_ref, f32[256,768]{1,0:T(8,128)S(1)} %get-tuple-element.35.refs_1_.refs_3_.refs_0_, f32[256,768]{1,0:T(8,128)S(1)} %collective-permute-done.15.refs_1_.refs_7_.refs_5_, ...), custom_call_target="tpu_custom_call", output_to_operand_aliasing={{}: (6, {})} | custom-call | flops 1811939328 | bytes 4718592 | tf_op jit(solution)/shard_map/tiles/pallas_call | solution.py:299
  88.9 3.7 %tiles.11.refs_8_ = f32[1536,6144]{1,0:T(8,128)} custom-call(bf16[1536,768]{1,0:T(8,128)(2,1)S(1)} %get-tuple-element.33.rows_ref, f32[256,768]{1,0:T(8,128)S(1)} %collective-permute-done.10.refs_2_.refs_3_.refs_0_, f32[256,768]{1,0:T(8,128)S(1)} %collective-permute-done.11.refs_1_.refs_4_, ...), custom_call_target="tpu_custom_call", output_to_operand_aliasing={{}: (9, {})} | custom-call | flops 3623878656 | bytes 9437184 | tf_op jit(solution)/shard_map/tiles/pallas_call | solution.py:299
  92.6 3.2 %collective-permute-done.18.refs_2_ = f32[256,768]{1,0:T(8,128)S(1)} collective-permute-done((f32[256,768]{1,0:T(8,128)S(1)}, f32[256,768]{1,0:T(8,128)S(1)}, u32[]{:S(2)}, u32[]{:S(2)}) %collective-permute-start.18) | collective-permute-done | bytes 786464 | tf_op jit(solution)/shard_map/ppermute | solution.py:389
  95.8 11.8 %collective-permute-start.20 = (f32[128,768]{1,0:T(8,128)S(1)}, f32[128,768]{1,0:T(8,128)S(1)}, u32[]{:S(2)}, u32[]{:S(2)}) collective-permute-start(f32[128,768]{1,0:T(8,128)S(1)} %slice.14), channel_id=1, source_target_pairs={{12,14},{14,10},{11,7},{7,3},{3,1},{1,5},{4,8},{8,12},{28,30},{30,... | collective-permute-start | bytes 1179656 | tf_op jit(solution)/shard_map/ppermute | solution.py:389
  107.6 1.3 collective-permute-start.21
  108.9 4.6 %collective-permute-start.16 = (f32[128,768]{1,0:T(8,128)S(1)}, f32[128,768]{1,0:T(8,128)S(1)}, u32[]{:S(2)}, u32[]{:S(2)}) collective-permute-start(f32[128,768]{1,0:T(8,128)S(1)} %slice.12), channel_id=1, source_target_pairs={{12,14},{14,10},{11,7},{7,3},{3,1},{1,5},{4,8},{8,12},{28,30},{30,... | collective-permute-start | bytes 1179656 | tf_op jit(solution)/shard_map/ppermute | solution.py:389
  113.5 1.3 collective-permute-start.17
  114.8 3.5 %tiles.12.refs_4_ = f32[1536,6144]{1,0:T(8,128)} custom-call(bf16[1536,768]{1,0:T(8,128)(2,1)S(1)} %get-tuple-element.33.rows_ref, f32[256,768]{1,0:T(8,128)S(1)} %collective-permute-done.8.refs_2_.refs_4_.refs_0_, f32[256,768]{1,0:T(8,128)S(1)} %collective-permute-done.14.refs_2_.refs_5_.refs_1_, ...), custom_call_target="tpu_custom_call", output_to_operand_aliasing={{}: (9, {})} | custom-call | flops 3623878656 | bytes 9437184 | tf_op jit(solution)/shard_map/tiles/pallas_call | solution.py:299
  118.7 4.4 %collective-permute-done.17.refs_1_ = f32[128,768]{1,0:T(8,128)S(1)} collective-permute-done((f32[128,768]{1,0:T(8,128)S(1)}, f32[128,768]{1,0:T(8,128)S(1)}, u32[]{:S(2)}, u32[]{:S(2)}) %collective-permute-start.17) | collective-permute-done | bytes 393248 | tf_op jit(solution)/shard_map/ppermute | solution.py:389
  123.1 6.1 %tiles.13 = f32[1536,6144]{1,0:T(8,128)} custom-call(bf16[1536,768]{1,0:T(8,128)(2,1)S(1)} %get-tuple-element.33.rows_ref, f32[128,768]{1,0:T(8,128)S(1)} %collective-permute-done.16.refs_0_, f32[128,768]{1,0:T(8,128)S(1)} %collective-permute-done.17.refs_1_, f32[128,768]{1,0:T(8,128)S(1)} %collective-permute-done.20.refs_2_, ...), custom_call_target="tpu_custom_call", output_to_operand_aliasing={{}: (5, {})} | custom-call | flops 3623878656 | bytes 9437184 | tf_op jit(solution)/shard_map/tiles/pallas_call | solution.py:299
  (30 shorter events, 5.6 us)
Async XLA Ops:
  0.0 5.0 %collective-permute-start = (f32[1,32,256]{2,1,0:T(8,128)}, f32[1,32,256]{2,1,0:T(8,128)S(1)}, u32[]{:S(2)}, u32[]{:S(2)}) collective-permute-start(f32[1,32,256]{2,1,0:T(8,128)} %bitcast.1), channel_id=1, source_target_pairs={{0,8},{1,9},{2,10},{3,11},{4,12},{5,13},{6,14},{7,15},{8,0},{9,1},... | collective-permute-start | bytes 98312 | tf_op jit(solution)/shard_map/ppermute | solution.py:327
  0.3 50.3 %collective-permute-start.6 = (f32[768,512]{1,0:T(8,128)}, f32[768,512]{1,0:T(8,128)S(1)}, u32[]{:S(2)}, u32[]{:S(2)}) collective-permute-start(f32[768,512]{1,0:T(8,128)} %slab_ref.1), channel_id=1, source_target_pairs={{0,4},{4,8},{8,13},{12,15},{14,11},{10,7},{6,2},{2,0},{16,20},{20,... | collective-permute-start | bytes 4718600 | tf_op jit(solution)/shard_map/ppermute | solution.py:389
  3.0 47.6 %collective-permute-start.7 = (f32[768,512]{1,0:T(8,128)}, f32[768,512]{1,0:T(8,128)S(1)}, u32[]{:S(2)}, u32[]{:S(2)}) collective-permute-start(f32[768,512]{1,0:T(8,128)} %slab_ref.1), channel_id=1, source_target_pairs={{0,2},{4,0},{8,5},{12,9},{14,13},{10,15},{6,10},{2,6},{16,18},{20,... | collective-permute-start | bytes 4718600 | tf_op jit(solution)/shard_map/ppermute | solution.py:389
  5.8 19.6 %collective-permute-start.1 = (f32[2,32,256]{2,1,0:T(8,128)S(1)}, f32[2,32,256]{2,1,0:T(8,128)S(1)}, u32[]{:S(2)}, u32[]{:S(2)}) collective-permute-start(f32[2,32,256]{2,1,0:T(8,128)S(1)} %pad_maximum_fusion.1), channel_id=1, source_target_pairs={{0,4},{1,5},{2,6},{3,7},{4,0},{5,1},{6,2},{7,3},{8,12},{9,13},{10,... | collective-permute-start | bytes 196616 | tf_op jit(solution)/shard_map/ppermute | solution.py:327
  7.6 49.0 %collective-permute-start.5 = (f32[768,512]{1,0:T(8,128)}, f32[768,512]{1,0:T(8,128)S(1)}, u32[]{:S(2)}, u32[]{:S(2)}) collective-permute-start(f32[768,512]{1,0:T(8,128)} %slab_ref.1), channel_id=1, source_target_pairs={{0,1},{1,0},{2,3},{3,2},{4,5},{5,4},{6,7},{7,6},{8,9},{9,8},{10,11... | collective-permute-start | bytes 4718600 | tf_op jit(solution)/shard_map/ppermute | solution.py:420
  26.2 5.0 %collective-permute-start.2 = (f32[4,32,256]{2,1,0:T(8,128)S(1)}, f32[4,32,256]{2,1,0:T(8,128)S(1)}, u32[]{:S(2)}, u32[]{:S(2)}) collective-permute-start(f32[4,32,256]{2,1,0:T(8,128)S(1)} %pad_maximum_fusion.refs_0_), channel_id=1, source_target_pairs={{0,2},{1,3},{2,0},{3,1},{4,6},{5,7},{6,4},{7,5},{8,10},{9,11},{10,... | collective-permute-start | bytes 393224 | tf_op jit(solution)/shard_map/ppermute | solution.py:330
  27.3 3.9 %collective-permute-start.3 = (f32[4,32,256]{2,1,0:T(8,128)S(1)}, f32[4,32,256]{2,1,0:T(8,128)S(1)}, u32[]{:S(2)}, u32[]{:S(2)}) collective-permute-start(f32[4,32,256]{2,1,0:T(8,128)S(1)} %pad_maximum_fusion.refs_0_), channel_id=1, source_target_pairs={{0,1},{1,0},{2,3},{3,2},{4,5},{5,4},{6,7},{7,6},{8,9},{9,8},{10,11... | collective-permute-start | bytes 393224 | tf_op jit(solution)/shard_map/ppermute | solution.py:332
  31.2 1.3 %collective-permute-start.4 = (f32[4,32,256]{2,1,0:T(8,128)S(1)}, f32[4,32,256]{2,1,0:T(8,128)S(1)}, u32[]{:S(2)}, u32[]{:S(2)}) collective-permute-start(f32[4,32,256]{2,1,0:T(8,128)S(1)} %collective-permute-done.2.refs_1_), channel_id=1, source_target_pairs={{0,1},{1,0},{2,3},{3,2},{4,5},{5,4},{6,7},{7,6},{8,9},{9,8},{10,11... | collective-permute-start | bytes 393224 | tf_op jit(solution)/shard_map/ppermute | solution.py:333
  32.5 1.4 %copy-start = (f32[768,512]{1,0:T(8,128)S(1)}, f32[768,512]{1,0:T(8,128)}, u32[]{:S(2)}) copy-start(f32[768,512]{1,0:T(8,128)} %slab_ref.1) | copy-start | bytes 4718596
  48.6 15.6 %collective-permute-start.10 = (f32[256,768]{1,0:T(8,128)S(1)}, f32[256,768]{1,0:T(8,128)S(1)}, u32[]{:S(2)}, u32[]{:S(2)}) collective-permute-start(f32[256,768]{1,0:T(8,128)S(1)} %get-tuple-element.32.mine_ref.refs_0_), channel_id=1, source_target_pairs={{1,4},{5,8},{9,13},{13,15},{15,11},{11,7},{7,2},{3,0},{17,20},{21,... | collective-permute-start | bytes 2359304 | tf_op jit(solution)/shard_map/ppermute | solution.py:389
  49.9 14.3 %collective-permute-start.11 = (f32[256,768]{1,0:T(8,128)S(1)}, f32[256,768]{1,0:T(8,128)S(1)}, u32[]{:S(2)}, u32[]{:S(2)}) collective-permute-start(f32[256,768]{1,0:T(8,128)S(1)} %get-tuple-element.32.mine_ref.refs_0_), channel_id=1, source_target_pairs={{1,2},{5,0},{9,5},{13,9},{15,13},{11,15},{7,10},{3,6},{17,18},{21,... | collective-permute-start | bytes 2359304 | tf_op jit(solution)/shard_map/ppermute | solution.py:389
  53.0 17.2 %collective-permute-start.9 = (f32[256,768]{1,0:T(8,128)S(1)}, f32[256,768]{1,0:T(8,128)S(1)}, u32[]{:S(2)}, u32[]{:S(2)}) collective-permute-start(f32[256,768]{1,0:T(8,128)S(1)} %get-tuple-element.35.refs_1_.refs_3_.refs_0_), channel_id=1, source_target_pairs={{2,6},{0,2},{5,1},{9,5},{13,9},{15,13},{10,14},{6,10},{18,22},{16,... | collective-permute-start | bytes 2359304 | tf_op jit(solution)/shard_map/ppermute | solution.py:389
  53.7 16.8 %collective-permute-start.8 = (f32[256,768]{1,0:T(8,128)S(1)}, f32[256,768]{1,0:T(8,128)S(1)}, u32[]{:S(2)}, u32[]{:S(2)}) collective-permute-start(f32[256,768]{1,0:T(8,128)S(1)} %get-tuple-element.34.refs_2_.refs_0_), channel_id=1, source_target_pairs={{4,8},{8,12},{13,15},{15,11},{11,7},{7,3},{2,0},{0,4},{20,24},{24,... | collective-permute-start | bytes 2359304 | tf_op jit(solution)/shard_map/ppermute | solution.py:389
  64.2 14.7 %collective-permute-start.14 = (f32[256,768]{1,0:T(8,128)S(1)}, f32[256,768]{1,0:T(8,128)S(1)}, u32[]{:S(2)}, u32[]{:S(2)}) collective-permute-start(f32[256,768]{1,0:T(8,128)S(1)} %collective-permute-done.10.refs_2_.refs_3_.refs_0_), channel_id=1, source_target_pairs={{4,8},{8,12},{13,15},{15,11},{11,7},{7,3},{2,0},{0,4},{20,24},{24,... | collective-permute-start | bytes 2359304 | tf_op jit(solution)/shard_map/ppermute | solution.py:389
  66.1 12.8 %collective-permute-start.15 = (f32[256,768]{1,0:T(8,128)S(1)}, f32[256,768]{1,0:T(8,128)S(1)}, u32[]{:S(2)}, u32[]{:S(2)}) collective-permute-start(f32[256,768]{1,0:T(8,128)S(1)} %collective-permute-done.11.refs_1_.refs_4_), channel_id=1, source_target_pairs={{2,6},{0,2},{5,1},{9,5},{13,9},{15,13},{10,14},{6,10},{18,22},{16,... | collective-permute-start | bytes 2359304 | tf_op jit(solution)/shard_map/ppermute | solution.py:389
  70.5 18.3 %collective-permute-start.12 = (f32[256,768]{1,0:T(8,128)S(1)}, f32[256,768]{1,0:T(8,128)S(1)}, u32[]{:S(2)}, u32[]{:S(2)}) collective-permute-start(f32[256,768]{1,0:T(8,128)S(1)} %collective-permute-done.8.refs_2_.refs_4_.refs_0_), channel_id=1, source_target_pairs={{8,12},{12,14},{15,11},{11,7},{7,3},{3,1},{0,4},{4,8},{24,28},{28,... | collective-permute-start | bytes 2359304 | tf_op jit(solution)/shard_map/ppermute | solution.py:389
  73.5 15.4 %collective-permute-start.13 = (f32[256,768]{1,0:T(8,128)S(1)}, f32[256,768]{1,0:T(8,128)S(1)}, u32[]{:S(2)}, u32[]{:S(2)}) collective-permute-start(f32[256,768]{1,0:T(8,128)S(1)} %collective-permute-done.9.refs_1_.refs_6_.refs_4_), channel_id=1, source_target_pairs={{6,10},{2,6},{1,3},{5,1},{9,5},{13,9},{14,12},{10,14},{22,26},{18,... | collective-permute-start | bytes 2359304 | tf_op jit(solution)/shard_map/ppermute | solution.py:389
  78.9 16.8 %collective-permute-start.18 = (f32[256,768]{1,0:T(8,128)S(1)}, f32[256,768]{1,0:T(8,128)S(1)}, u32[]{:S(2)}, u32[]{:S(2)}) collective-permute-start(f32[256,768]{1,0:T(8,128)S(1)} %collective-permute-done.14.refs_2_.refs_5_.refs_1_), channel_id=1, source_target_pairs={{8,12},{12,14},{15,11},{11,7},{7,3},{3,1},{0,4},{4,8},{24,28},{28,... | collective-permute-start | bytes 2359304 | tf_op jit(solution)/shard_map/ppermute | solution.py:389
  84.7 11.1 %collective-permute-start.19 = (f32[256,768]{1,0:T(8,128)S(1)}, f32[256,768]{1,0:T(8,128)S(1)}, u32[]{:S(2)}, u32[]{:S(2)}) collective-permute-start(f32[256,768]{1,0:T(8,128)S(1)} %collective-permute-done.15.refs_1_.refs_7_.refs_5_), channel_id=1, source_target_pairs={{6,10},{2,6},{1,3},{5,1},{9,5},{13,9},{14,12},{10,14},{22,26},{18,... | collective-permute-start | bytes 2359304 | tf_op jit(solution)/shard_map/ppermute | solution.py:389
  95.8 22.4 %collective-permute-start.20 = (f32[128,768]{1,0:T(8,128)S(1)}, f32[128,768]{1,0:T(8,128)S(1)}, u32[]{:S(2)}, u32[]{:S(2)}) collective-permute-start(f32[128,768]{1,0:T(8,128)S(1)} %slice.14), channel_id=1, source_target_pairs={{12,14},{14,10},{11,7},{7,3},{3,1},{1,5},{4,8},{8,12},{28,30},{30,... | collective-permute-start | bytes 1179656 | tf_op jit(solution)/shard_map/ppermute | solution.py:389
  107.6 10.6 %collective-permute-start.21 = (f32[128,768]{1,0:T(8,128)S(1)}, f32[128,768]{1,0:T(8,128)S(1)}, u32[]{:S(2)}, u32[]{:S(2)}) collective-permute-start(f32[128,768]{1,0:T(8,128)S(1)} %slice.15), channel_id=1, source_target_pairs={{10,14},{6,10},{3,7},{1,3},{5,1},{9,5},{12,8},{14,12},{26,30},{22,... | collective-permute-start | bytes 1179656 | tf_op jit(solution)/shard_map/ppermute | solution.py:389
  108.9 9.8 %collective-permute-start.16 = (f32[128,768]{1,0:T(8,128)S(1)}, f32[128,768]{1,0:T(8,128)S(1)}, u32[]{:S(2)}, u32[]{:S(2)}) collective-permute-start(f32[128,768]{1,0:T(8,128)S(1)} %slice.12), channel_id=1, source_target_pairs={{12,14},{14,10},{11,7},{7,3},{3,1},{1,5},{4,8},{8,12},{28,30},{30,... | collective-permute-start | bytes 1179656 | tf_op jit(solution)/shard_map/ppermute | solution.py:389
  113.5 9.7 %collective-permute-start.17 = (f32[128,768]{1,0:T(8,128)S(1)}, f32[128,768]{1,0:T(8,128)S(1)}, u32[]{:S(2)}, u32[]{:S(2)}) collective-permute-start(f32[128,768]{1,0:T(8,128)S(1)} %slice.13), channel_id=1, source_target_pairs={{10,14},{6,10},{3,7},{1,3},{5,1},{9,5},{12,8},{14,12},{26,30},{22,... | collective-permute-start | bytes 1179656 | tf_op jit(solution)/shard_map/ppermute | solution.py:389

commit v2 on v1

--- a/solution.py
+++ b/solution.py
@@ -293,7 +293,7 @@
     turns = plan.shape[1] // 2
     k, shard = rows.shape[1] // 3, pieces[0][0].shape[1]
     arrays = [w for piece in pieces for w in piece]
-    steps = 3 if rows.shape[0] % 48 == 0 else 2
+    steps = 4 if rows.shape[0] % 64 == 0 else 2
     height = rows.shape[0] // steps
     given = [] if out is None else [out]
     return pl.pallas_call(
@@ -426,8 +426,8 @@
         if steps + 1 < half:
             flights.append((core, steps + 1, {way: hop(sent[way], way, steps + 1) for way in sent}))
         elif steps + 1 == half:
-            k = sent[1].shape[0] // 2
-            flights.append((core, half, {1: hop(sent[1][:k], 1, half), -1: hop(sent[-1][k:], -1, half)}))
+            way = (1, -1)[core]
+            flights.append((core, half, {way: hop(sent[way], way, half)}))
 
     onward(0, 1, first)
     rows, theirs = own_parts(comp, mine, other)
@@ -435,23 +435,18 @@
     arrive(0, "theirs", [theirs])
     for way in (1, -1):
         arrive(-way, 0, [first[way]])
-    out = work(rows, None, 1)
+    out = None
     while flights:
         core, steps, sent = flights.pop(0)
-        if steps == half and flights:
-            core, steps, sent = core, half, {(c, way): w for c, _, ws in [(core, half, sent)] + flights for way, w in ws.items()}
-            flights.clear()
-        got = lax.optimization_barrier(tuple(sent.values()) + (out,))
-        out = got[-1]
-        sent = dict(zip(sent, got))
+        needed = [(1, -1)[core]] if steps + 1 == half else list(sent)
+        got = lax.optimization_barrier(tuple(sent[way] for way in needed) + (rows if out is None else out,))
+        turns = 1 if steps + 1 < half and out is not None else 2
+        rows, out = (got[-1], None) if out is None else (rows, got[-1])
+        sent.update(zip(needed, got))
         onward(core, steps, sent)
-        if steps < half:
-            for way, w in sent.items():
-                arrive(-way * steps, core, [w])
-        else:
-            for c in range(n_col):
-                arrive(half, c, [sent[c, 1], sent[c, -1]])
-        out = work(rows, out, (1 if steps + 1 < half else 2) if flights else 8)
+        for way, w in sent.items():
+            arrive(half if steps == half else -way * steps, core, [w])
+        out = work(rows, out, turns if flights else 8)
     return out
 
 

time: 130 us -> 122 us (0.938)
  the two profiles are of different devices: /device:TPU:20 before, /device:TPU:28 now
where the time goes in v2:
time: 122 us; the launch traced here: 121 us
  Pallas kernels  42.2 us (35%)
  waiting for transfers between devices  40.7 us (33%)
  starting transfers between devices  35 us (29%)
  other arithmetic  1.53 us (1%)
  local copies, waits for them, and re-layouts  1.41 us (1%)
    ppermute x14, starting transfers between devices, hop(): return lax.ppermute(x, AXES, pairs)  30.1 us
    pallas_call x7, Pallas kernels, tiles(): pl.pallas_call(functools.partial(tiles_kernel, [len(piece) for piece in p...  24.3 us
    ppermute x14, waiting for transfers between devices, hop(): return lax.ppermute(x, AXES, pairs)  18.7 us
    ppermute x2, waiting for transfers between devices, gather_all(): other = lax.ppermute(y, AXES, [(i, i ^ bit) for i in range(n)])  18.1 us
    pallas_call x1, Pallas kernels, basis(): pl.pallas_call(functools.partial(basis_kernel, len(parts), spots), out_sh...  14.6 us
    ppermute x1, starting transfers between devices, gather_all(): far = lax.ppermute(y, AXES, [(i, i ^ bit) for i in range(n)])  3.9 us
    ppermute x1, waiting for transfers between devices, gather_all(): far = lax.ppermute(y, AXES, [(i, i ^ bit) for i in range(n)])  2.94 us
  transfers between devices with their start and end apart: 20, of which 8 were waited for; matrix products, arithmetic and copies ran while one was open for 1% of the time, Pallas kernels for 32%

profile of v2, /device:TPU:28, one launch (start us, length us, event | category | flops | bytes accessed | tf_op | source)
XLA Modules:
  0.0 121.3 jit_solution(13681382837977546672)
XLA Ops:
  0.3 2.6 %collective-permute-start.10 = (f32[768,512]{1,0:T(8,128)}, f32[768,512]{1,0:T(8,128)S(1)}, u32[]{:S(2)}, u32[]{:S(2)}) collective-permute-start(f32[768,512]{1,0:T(8,128)} %slab_ref.1), channel_id=1, source_target_pairs={{0,4},{4,8},{8,13},{12,15},{14,11},{10,7},{6,2},{2,0},{16,20},{20,... | collective-permute-start | bytes 4718600 | tf_op jit(solution)/shard_map/ppermute | solution.py:389
  3.0 1.4 %collective-permute-start.11 = (f32[768,512]{1,0:T(8,128)}, f32[768,512]{1,0:T(8,128)S(1)}, u32[]{:S(2)}, u32[]{:S(2)}) collective-permute-start(f32[768,512]{1,0:T(8,128)} %slab_ref.1), channel_id=1, source_target_pairs={{0,2},{4,0},{8,5},{12,9},{14,13},{10,15},{6,10},{2,6},{16,18},{20,... | collective-permute-start | bytes 4718600 | tf_op jit(solution)/shard_map/ppermute | solution.py:389
  4.4 0.9 collective-permute-done
  5.3 0.8 pad_maximum_fusion.1
  6.3 17.3 %collective-permute-done.1 = f32[2,32,256]{2,1,0:T(8,128)S(1)} collective-permute-done((f32[2,32,256]{2,1,0:T(8,128)S(1)}, f32[2,32,256]{2,1,0:T(8,128)S(1)}, u32[]{:S(2)}, u32[]{:S(2)}) %collective-permute-start.1) | collective-permute-done | bytes 65568 | tf_op jit(solution)/shard_map/ppermute | solution.py:327
  23.5 0.8 pad_maximum_fusion.refs_0_
  24.3 3.9 %collective-permute-start.2 = (f32[4,32,256]{2,1,0:T(8,128)S(1)}, f32[4,32,256]{2,1,0:T(8,128)S(1)}, u32[]{:S(2)}, u32[]{:S(2)}) collective-permute-start(f32[4,32,256]{2,1,0:T(8,128)S(1)} %pad_maximum_fusion.refs_0_), channel_id=1, source_target_pairs={{0,2},{1,3},{2,0},{3,1},{4,6},{5,7},{6,4},{7,5},{8,10},{9,11},{10,... | collective-permute-start | bytes 393224 | tf_op jit(solution)/shard_map/ppermute | solution.py:330
  28.2 2.9 %collective-permute-done.2.refs_1_ = f32[4,32,256]{2,1,0:T(8,128)S(1)} collective-permute-done((f32[4,32,256]{2,1,0:T(8,128)S(1)}, f32[4,32,256]{2,1,0:T(8,128)S(1)}, u32[]{:S(2)}, u32[]{:S(2)}) %collective-permute-start.2) | collective-permute-done | bytes 131104 | tf_op jit(solution)/shard_map/ppermute | solution.py:330
  31.7 0.8 collective-permute-done.4.refs_3_
  32.5 1.4 %copy-done = f32[768,512]{1,0:T(8,128)S(1)} copy-done((f32[768,512]{1,0:T(8,128)S(1)}, f32[768,512]{1,0:T(8,128)}, u32[]{:S(2)}) %copy-start) | copy-done | bytes 1572888
  33.9 14.6 %basis.1 = (f32[256,512]{1,0:T(8,128)S(1)}, f32[256,768]{1,0:T(8,128)S(1)}) custom-call(f32[768,512]{1,0:T(8,128)S(1)} %copy-done, f32[4,32,256]{2,1,0:T(8,128)S(1)} %pad_maximum_fusion.refs_0_, f32[4,32,256]{2,1,0:T(8,128)S(1)} %collective-permute-done.2.refs_1_, f32[4,32,256]{2,1,0:T(8,128)S(1)} %collective-permute-done.3.refs_2_, ...), custom_call_target="tpu_custom_call" | custom-call | flops 8000000000 | bytes 1048576 | tf_op jit(solution)/shard_map/basis/pallas_call | solution.py:159
  48.5 0.7 collective-permute-start.5
  49.2 0.7 collective-permute-start.6
  50.0 2.4 %project.1 = (f32[256,768]{1,0:T(8,128)S(1)}, f32[256,768]{1,0:T(8,128)S(1)}) custom-call(f32[256,512]{1,0:T(8,128)S(1)} %get-tuple-element.29.c_ref, f32[768,512]{1,0:T(8,128)S(1)} %collective-permute-done.10.refs_0_, f32[768,512]{1,0:T(8,128)S(1)} %collective-permute-done.11.refs_1_), custom_call_target="tpu_custom_call" | custom-call | flops 1207959552 | bytes 4718592 | tf_op jit(solution)/shard_map/project/pallas_call | solution.py:202
  53.1 1.3 %collective-permute-start.12 = (f32[256,768]{1,0:T(8,128)S(1)}, f32[256,768]{1,0:T(8,128)S(1)}, u32[]{:S(2)}, u32[]{:S(2)}) collective-permute-start(f32[256,768]{1,0:T(8,128)S(1)} %get-tuple-element.34.refs_4_.refs_0_), channel_id=1, source_target_pairs={{4,8},{8,12},{13,15},{15,11},{11,7},{7,3},{2,0},{0,4},{20,24},{24,... | collective-permute-start | bytes 2359304 | tf_op jit(solution)/shard_map/ppermute | solution.py:389
  54.4 1.0 own.1
  55.4 1.3 %collective-permute-start.8 = (f32[256,768]{1,0:T(8,128)S(1)}, f32[256,768]{1,0:T(8,128)S(1)}, u32[]{:S(2)}, u32[]{:S(2)}) collective-permute-start(f32[256,768]{1,0:T(8,128)S(1)} %collective-permute-done.5.refs_5_.refs_3_.refs_0_), channel_id=1, source_target_pairs={{4,8},{8,12},{13,15},{15,11},{11,7},{7,3},{2,0},{0,4},{20,24},{24,... | collective-permute-start | bytes 2359304 | tf_op jit(solution)/shard_map/ppermute | solution.py:389
  57.6 12.4 %collective-permute-done.12.refs_2_.refs_4_.refs_0_ = f32[256,768]{1,0:T(8,128)S(1)} collective-permute-done((f32[256,768]{1,0:T(8,128)S(1)}, f32[256,768]{1,0:T(8,128)S(1)}, u32[]{:S(2)}, u32[]{:S(2)}) %collective-permute-start.12) | collective-permute-done | bytes 786464 | tf_op jit(solution)/shard_map/ppermute | solution.py:389
  70.0 6.5 %collective-permute-start.15 = (f32[256,768]{1,0:T(8,128)S(1)}, f32[256,768]{1,0:T(8,128)S(1)}, u32[]{:S(2)}, u32[]{:S(2)}) collective-permute-start(f32[256,768]{1,0:T(8,128)S(1)} %collective-permute-done.12.refs_2_.refs_4_.refs_0_), channel_id=1, source_target_pairs={{8,12},{12,14},{15,11},{11,7},{7,3},{3,1},{0,4},{4,8},{24,28},{28,... | collective-permute-start | bytes 2359304 | tf_op jit(solution)/shard_map/ppermute | solution.py:389
  76.5 1.3 %collective-permute-start.16 = (f32[256,768]{1,0:T(8,128)S(1)}, f32[256,768]{1,0:T(8,128)S(1)}, u32[]{:S(2)}, u32[]{:S(2)}) collective-permute-start(f32[256,768]{1,0:T(8,128)S(1)} %collective-permute-done.13.refs_1_.refs_6_.refs_4_), channel_id=1, source_target_pairs={{6,10},{2,6},{1,3},{5,1},{9,5},{13,9},{14,12},{10,14},{22,26},{18,... | collective-permute-start | bytes 2359304 | tf_op jit(solution)/shard_map/ppermute | solution.py:389
  77.8 3.3 %tiles.8.refs_5_ = f32[1536,6144]{1,0:T(8,128)} custom-call(bf16[1536,768]{1,0:T(8,128)(2,1)S(1)} %get-tuple-element.31.rows_ref, f32[256,768]{1,0:T(8,128)S(1)} %get-tuple-element.34.refs_4_.refs_0_, f32[256,768]{1,0:T(8,128)S(1)} %collective-permute-done.13.refs_1_.refs_6_.refs_4_, ...), custom_call_target="tpu_custom_call", output_to_operand_aliasing={{}: (5, {})} | custom-call | flops 1811939328 | bytes 4718592 | tf_op jit(solution)/shard_map/tiles/pallas_call | solution.py:299
  81.1 1.3 %collective-permute-start.14 = (f32[256,768]{1,0:T(8,128)S(1)}, f32[256,768]{1,0:T(8,128)S(1)}, u32[]{:S(2)}, u32[]{:S(2)}) collective-permute-start(f32[256,768]{1,0:T(8,128)S(1)} %collective-permute-done.9.refs_1_.refs_7_.refs_5_), channel_id=1, source_target_pairs={{6,10},{2,6},{1,3},{5,1},{9,5},{13,9},{14,12},{10,14},{22,26},{18,... | collective-permute-start | bytes 2359304 | tf_op jit(solution)/shard_map/ppermute | solution.py:389
  82.4 5.2 %collective-permute-start.19 = (f32[256,768]{1,0:T(8,128)S(1)}, f32[256,768]{1,0:T(8,128)S(1)}, u32[]{:S(2)}, u32[]{:S(2)}) collective-permute-start(f32[256,768]{1,0:T(8,128)S(1)} %collective-permute-done.8.refs_2_.refs_5_.refs_1_), channel_id=1, source_target_pairs={{8,12},{12,14},{15,11},{11,7},{7,3},{3,1},{0,4},{4,8},{24,28},{28,... | collective-permute-start | bytes 2359304 | tf_op jit(solution)/shard_map/ppermute | solution.py:389
  87.6 3.5 %tiles.9.refs_8_ = f32[1536,6144]{1,0:T(8,128)} custom-call(bf16[1536,768]{1,0:T(8,128)(2,1)S(1)} %get-tuple-element.31.rows_ref, f32[256,768]{1,0:T(8,128)S(1)} %get-tuple-element.35.refs_2_.refs_3_.refs_0_, f32[256,768]{1,0:T(8,128)S(1)} %collective-permute-done.9.refs_1_.refs_7_.refs_5_, ...), custom_call_target="tpu_custom_call", output_to_operand_aliasing={{}: (6, {})} | custom-call | flops 1811939328 | bytes 4718592 | tf_op jit(solution)/shard_map/tiles/pallas_call | solution.py:299
  91.5 4.4 %collective-permute-start.18 = (f32[256,768]{1,0:T(8,128)S(1)}, f32[256,768]{1,0:T(8,128)S(1)}, u32[]{:S(2)}, u32[]{:S(2)}) collective-permute-start(f32[256,768]{1,0:T(8,128)S(1)} %collective-permute-done.15.refs_2_.refs_6_), channel_id=1, source_target_pairs={{12,14},{14,10},{11,7},{7,3},{3,1},{1,5},{4,8},{8,12},{28,30},{30,... | collective-permute-start | bytes 2359304 | tf_op jit(solution)/shard_map/ppermute | solution.py:389
  95.9 5.4 %tiles.10.refs_8_ = f32[1536,6144]{1,0:T(8,128)} custom-call(bf16[1536,768]{1,0:T(8,128)(2,1)S(1)} %get-tuple-element.31.rows_ref, f32[256,768]{1,0:T(8,128)S(1)} %collective-permute-done.5.refs_5_.refs_3_.refs_0_, f32[256,768]{1,0:T(8,128)S(1)} %collective-permute-done.6.refs_3_.refs_4_.refs_1_, ...), custom_call_target="tpu_custom_call", output_to_operand_aliasing={{}: (9, {})} | custom-call | flops 3623878656 | bytes 9437184 | tf_op jit(solution)/shard_map/tiles/pallas_call | solution.py:299
  101.3 2.8 %collective-permute-done.14.refs_3_ = f32[256,768]{1,0:T(8,128)S(1)} collective-permute-done((f32[256,768]{1,0:T(8,128)S(1)}, f32[256,768]{1,0:T(8,128)S(1)}, u32[]{:S(2)}, u32[]{:S(2)}) %collective-permute-start.14) | collective-permute-done | bytes 786464 | tf_op jit(solution)/shard_map/ppermute | solution.py:389
  104.0 1.9 %collective-permute-start.17 = (f32[256,768]{1,0:T(8,128)S(1)}, f32[256,768]{1,0:T(8,128)S(1)}, u32[]{:S(2)}, u32[]{:S(2)}) collective-permute-start(f32[256,768]{1,0:T(8,128)S(1)} %collective-permute-done.14.refs_3_), channel_id=1, source_target_pairs={{10,14},{6,10},{3,7},{1,3},{5,1},{9,5},{12,8},{14,12},{26,30},{22,... | collective-permute-start | bytes 2359304 | tf_op jit(solution)/shard_map/ppermute | solution.py:389
  106.0 5.4 %tiles.11.refs_1_ = f32[1536,6144]{1,0:T(8,128)} custom-call(bf16[1536,768]{1,0:T(8,128)(2,1)S(1)} %get-tuple-element.31.rows_ref, f32[256,768]{1,0:T(8,128)S(1)} %collective-permute-done.12.refs_2_.refs_4_.refs_0_, f32[256,768]{1,0:T(8,128)S(1)} %collective-permute-done.8.refs_2_.refs_5_.refs_1_, ...), custom_call_target="tpu_custom_call", output_to_operand_aliasing={{}: (9, {})} | custom-call | flops 3623878656 | bytes 9437184 | tf_op jit(solution)/shard_map/tiles/pallas_call | solution.py:299
  111.4 3.2 %tiles.12.refs_1_ = f32[1536,6144]{1,0:T(8,128)} custom-call(bf16[1536,768]{1,0:T(8,128)(2,1)S(1)} %get-tuple-element.31.rows_ref, f32[256,768]{1,0:T(8,128)S(1)} %collective-permute-done.18.refs_0_, f32[1536,6144]{1,0:T(8,128)} %tiles.11.refs_1_), custom_call_target="tpu_custom_call", output_to_operand_aliasing={{}: (2, {})} | custom-call | flops 1811939328 | bytes 4718592 | tf_op jit(solution)/shard_map/tiles/pallas_call | solution.py:299
  114.7 3.2 %collective-permute-done.17.refs_0_ = f32[256,768]{1,0:T(8,128)S(1)} collective-permute-done((f32[256,768]{1,0:T(8,128)S(1)}, f32[256,768]{1,0:T(8,128)S(1)}, u32[]{:S(2)}, u32[]{:S(2)}) %collective-permute-start.17) | collective-permute-done | bytes 786464 | tf_op jit(solution)/shard_map/ppermute | solution.py:389
  117.9 3.2 %tiles.13 = f32[1536,6144]{1,0:T(8,128)} custom-call(bf16[1536,768]{1,0:T(8,128)(2,1)S(1)} %get-tuple-element.31.rows_ref, f32[256,768]{1,0:T(8,128)S(1)} %collective-permute-done.17.refs_0_, f32[1536,6144]{1,0:T(8,128)} %tiles.12.refs_1_), custom_call_target="tpu_custom_call", output_to_operand_aliasing={{}: (2, {})} | custom-call | flops 1811939328 | bytes 4718592 | tf_op jit(solution)/shard_map/tiles/pallas_call | solution.py:299
  (22 shorter events, 3.0 us)
Async XLA Ops:
  0.0 5.3 %collective-permute-start = (f32[1,32,256]{2,1,0:T(8,128)}, f32[1,32,256]{2,1,0:T(8,128)S(1)}, u32[]{:S(2)}, u32[]{:S(2)}) collective-permute-start(f32[1,32,256]{2,1,0:T(8,128)} %bitcast.1), channel_id=1, source_target_pairs={{0,8},{1,9},{2,10},{3,11},{4,12},{5,13},{6,14},{7,15},{8,0},{9,1},... | collective-permute-start | bytes 98312 | tf_op jit(solution)/shard_map/ppermute | solution.py:327
  0.3 49.6 %collective-permute-start.10 = (f32[768,512]{1,0:T(8,128)}, f32[768,512]{1,0:T(8,128)S(1)}, u32[]{:S(2)}, u32[]{:S(2)}) collective-permute-start(f32[768,512]{1,0:T(8,128)} %slab_ref.1), channel_id=1, source_target_pairs={{0,4},{4,8},{8,13},{12,15},{14,11},{10,7},{6,2},{2,0},{16,20},{20,... | collective-permute-start | bytes 4718600 | tf_op jit(solution)/shard_map/ppermute | solution.py:389
  3.0 47.0 %collective-permute-start.11 = (f32[768,512]{1,0:T(8,128)}, f32[768,512]{1,0:T(8,128)S(1)}, u32[]{:S(2)}, u32[]{:S(2)}) collective-permute-start(f32[768,512]{1,0:T(8,128)} %slab_ref.1), channel_id=1, source_target_pairs={{0,2},{4,0},{8,5},{12,9},{14,13},{10,15},{6,10},{2,6},{16,18},{20,... | collective-permute-start | bytes 4718600 | tf_op jit(solution)/shard_map/ppermute | solution.py:389
  6.0 17.5 %collective-permute-start.1 = (f32[2,32,256]{2,1,0:T(8,128)S(1)}, f32[2,32,256]{2,1,0:T(8,128)S(1)}, u32[]{:S(2)}, u32[]{:S(2)}) collective-permute-start(f32[2,32,256]{2,1,0:T(8,128)S(1)} %pad_maximum_fusion.1), channel_id=1, source_target_pairs={{0,4},{1,5},{2,6},{3,7},{4,0},{5,1},{6,2},{7,3},{8,12},{9,13},{10,... | collective-permute-start | bytes 196616 | tf_op jit(solution)/shard_map/ppermute | solution.py:327
  24.3 6.8 %collective-permute-start.2 = (f32[4,32,256]{2,1,0:T(8,128)S(1)}, f32[4,32,256]{2,1,0:T(8,128)S(1)}, u32[]{:S(2)}, u32[]{:S(2)}) collective-permute-start(f32[4,32,256]{2,1,0:T(8,128)S(1)} %pad_maximum_fusion.refs_0_), channel_id=1, source_target_pairs={{0,2},{1,3},{2,0},{3,1},{4,6},{5,7},{6,4},{7,5},{8,10},{9,11},{10,... | collective-permute-start | bytes 393224 | tf_op jit(solution)/shard_map/ppermute | solution.py:330
  28.2 3.5 %collective-permute-start.3 = (f32[4,32,256]{2,1,0:T(8,128)S(1)}, f32[4,32,256]{2,1,0:T(8,128)S(1)}, u32[]{:S(2)}, u32[]{:S(2)}) collective-permute-start(f32[4,32,256]{2,1,0:T(8,128)S(1)} %pad_maximum_fusion.refs_0_), channel_id=1, source_target_pairs={{0,1},{1,0},{2,3},{3,2},{4,5},{5,4},{6,7},{7,6},{8,9},{9,8},{10,11... | collective-permute-start | bytes 393224 | tf_op jit(solution)/shard_map/ppermute | solution.py:332
  31.1 1.3 %collective-permute-start.4 = (f32[4,32,256]{2,1,0:T(8,128)S(1)}, f32[4,32,256]{2,1,0:T(8,128)S(1)}, u32[]{:S(2)}, u32[]{:S(2)}) collective-permute-start(f32[4,32,256]{2,1,0:T(8,128)S(1)} %collective-permute-done.2.refs_1_), channel_id=1, source_target_pairs={{0,1},{1,0},{2,3},{3,2},{4,5},{5,4},{6,7},{7,6},{8,9},{9,8},{10,11... | collective-permute-start | bytes 393224 | tf_op jit(solution)/shard_map/ppermute | solution.py:333
  31.1 23.2 %collective-permute-start.7 = (f32[768,512]{1,0:T(8,128)}, f32[768,512]{1,0:T(8,128)S(1)}, u32[]{:S(2)}, u32[]{:S(2)}) collective-permute-start(f32[768,512]{1,0:T(8,128)} %slab_ref.1), channel_id=1, source_target_pairs={{0,1},{1,0},{2,3},{3,2},{4,5},{5,4},{6,7},{7,6},{8,9},{9,8},{10,11... | collective-permute-start | bytes 4718600 | tf_op jit(solution)/shard_map/ppermute | solution.py:420
  32.5 1.4 %copy-start = (f32[768,512]{1,0:T(8,128)S(1)}, f32[768,512]{1,0:T(8,128)}, u32[]{:S(2)}) copy-start(f32[768,512]{1,0:T(8,128)} %slab_ref.1) | copy-start | bytes 4718596
  48.5 6.9 %collective-permute-start.5 = (f32[256,768]{1,0:T(8,128)S(1)}, f32[256,768]{1,0:T(8,128)S(1)}, u32[]{:S(2)}, u32[]{:S(2)}) collective-permute-start(f32[256,768]{1,0:T(8,128)S(1)} %get-tuple-element.28.mine_ref.refs_0_), channel_id=1, source_target_pairs={{1,4},{5,8},{9,13},{13,15},{15,11},{11,7},{7,2},{3,0},{17,20},{21,... | collective-permute-start | bytes 2359304 | tf_op jit(solution)/shard_map/ppermute | solution.py:389
  49.2 6.2 %collective-permute-start.6 = (f32[256,768]{1,0:T(8,128)S(1)}, f32[256,768]{1,0:T(8,128)S(1)}, u32[]{:S(2)}, u32[]{:S(2)}) collective-permute-start(f32[256,768]{1,0:T(8,128)S(1)} %get-tuple-element.28.mine_ref.refs_0_), channel_id=1, source_target_pairs={{1,2},{5,0},{9,5},{13,9},{15,13},{11,15},{7,10},{3,6},{17,18},{21,... | collective-permute-start | bytes 2359304 | tf_op jit(solution)/shard_map/ppermute | solution.py:389
  52.3 5.2 %collective-permute-start.13 = (f32[256,768]{1,0:T(8,128)S(1)}, f32[256,768]{1,0:T(8,128)S(1)}, u32[]{:S(2)}, u32[]{:S(2)}) collective-permute-start(f32[256,768]{1,0:T(8,128)S(1)} %get-tuple-element.35.refs_2_.refs_3_.refs_0_), channel_id=1, source_target_pairs={{2,6},{0,2},{5,1},{9,5},{13,9},{15,13},{10,14},{6,10},{18,22},{16,... | collective-permute-start | bytes 2359304 | tf_op jit(solution)/shard_map/ppermute | solution.py:389
  53.1 16.9 %collective-permute-start.12 = (f32[256,768]{1,0:T(8,128)S(1)}, f32[256,768]{1,0:T(8,128)S(1)}, u32[]{:S(2)}, u32[]{:S(2)}) collective-permute-start(f32[256,768]{1,0:T(8,128)S(1)} %get-tuple-element.34.refs_4_.refs_0_), channel_id=1, source_target_pairs={{4,8},{8,12},{13,15},{15,11},{11,7},{7,3},{2,0},{0,4},{20,24},{24,... | collective-permute-start | bytes 2359304 | tf_op jit(solution)/shard_map/ppermute | solution.py:389
  55.4 25.7 %collective-permute-start.8 = (f32[256,768]{1,0:T(8,128)S(1)}, f32[256,768]{1,0:T(8,128)S(1)}, u32[]{:S(2)}, u32[]{:S(2)}) collective-permute-start(f32[256,768]{1,0:T(8,128)S(1)} %collective-permute-done.5.refs_5_.refs_3_.refs_0_), channel_id=1, source_target_pairs={{4,8},{8,12},{13,15},{15,11},{11,7},{7,3},{2,0},{0,4},{20,24},{24,... | collective-permute-start | bytes 2359304 | tf_op jit(solution)/shard_map/ppermute | solution.py:389
  56.7 24.4 %collective-permute-start.9 = (f32[256,768]{1,0:T(8,128)S(1)}, f32[256,768]{1,0:T(8,128)S(1)}, u32[]{:S(2)}, u32[]{:S(2)}) collective-permute-start(f32[256,768]{1,0:T(8,128)S(1)} %collective-permute-done.6.refs_3_.refs_4_.refs_1_), channel_id=1, source_target_pairs={{2,6},{0,2},{5,1},{9,5},{13,9},{15,13},{10,14},{6,10},{18,22},{16,... | collective-permute-start | bytes 2359304 | tf_op jit(solution)/shard_map/ppermute | solution.py:389
  70.0 21.5 %collective-permute-start.15 = (f32[256,768]{1,0:T(8,128)S(1)}, f32[256,768]{1,0:T(8,128)S(1)}, u32[]{:S(2)}, u32[]{:S(2)}) collective-permute-start(f32[256,768]{1,0:T(8,128)S(1)} %collective-permute-done.12.refs_2_.refs_4_.refs_0_), channel_id=1, source_target_pairs={{8,12},{12,14},{15,11},{11,7},{7,3},{3,1},{0,4},{4,8},{24,28},{28,... | collective-permute-start | bytes 2359304 | tf_op jit(solution)/shard_map/ppermute | solution.py:389
  76.5 19.3 %collective-permute-start.16 = (f32[256,768]{1,0:T(8,128)S(1)}, f32[256,768]{1,0:T(8,128)S(1)}, u32[]{:S(2)}, u32[]{:S(2)}) collective-permute-start(f32[256,768]{1,0:T(8,128)S(1)} %collective-permute-done.13.refs_1_.refs_6_.refs_4_), channel_id=1, source_target_pairs={{6,10},{2,6},{1,3},{5,1},{9,5},{13,9},{14,12},{10,14},{22,26},{18,... | collective-permute-start | bytes 2359304 | tf_op jit(solution)/shard_map/ppermute | solution.py:389
  81.1 23.0 %collective-permute-start.14 = (f32[256,768]{1,0:T(8,128)S(1)}, f32[256,768]{1,0:T(8,128)S(1)}, u32[]{:S(2)}, u32[]{:S(2)}) collective-permute-start(f32[256,768]{1,0:T(8,128)S(1)} %collective-permute-done.9.refs_1_.refs_7_.refs_5_), channel_id=1, source_target_pairs={{6,10},{2,6},{1,3},{5,1},{9,5},{13,9},{14,12},{10,14},{22,26},{18,... | collective-permute-start | bytes 2359304 | tf_op jit(solution)/shard_map/ppermute | solution.py:389
  82.4 23.6 %collective-permute-start.19 = (f32[256,768]{1,0:T(8,128)S(1)}, f32[256,768]{1,0:T(8,128)S(1)}, u32[]{:S(2)}, u32[]{:S(2)}) collective-permute-start(f32[256,768]{1,0:T(8,128)S(1)} %collective-permute-done.8.refs_2_.refs_5_.refs_1_), channel_id=1, source_target_pairs={{8,12},{12,14},{15,11},{11,7},{7,3},{3,1},{0,4},{4,8},{24,28},{28,... | collective-permute-start | bytes 2359304 | tf_op jit(solution)/shard_map/ppermute | solution.py:389
  91.5 20.0 %collective-permute-start.18 = (f32[256,768]{1,0:T(8,128)S(1)}, f32[256,768]{1,0:T(8,128)S(1)}, u32[]{:S(2)}, u32[]{:S(2)}) collective-permute-start(f32[256,768]{1,0:T(8,128)S(1)} %collective-permute-done.15.refs_2_.refs_6_), channel_id=1, source_target_pairs={{12,14},{14,10},{11,7},{7,3},{3,1},{1,5},{4,8},{8,12},{28,30},{30,... | collective-permute-start | bytes 2359304 | tf_op jit(solution)/shard_map/ppermute | solution.py:389
  104.0 13.9 %collective-permute-start.17 = (f32[256,768]{1,0:T(8,128)S(1)}, f32[256,768]{1,0:T(8,128)S(1)}, u32[]{:S(2)}, u32[]{:S(2)}) collective-permute-start(f32[256,768]{1,0:T(8,128)S(1)} %collective-permute-done.14.refs_3_), channel_id=1, source_target_pairs={{10,14},{6,10},{3,7},{1,3},{5,1},{9,5},{12,8},{14,12},{26,30},{22,... | collective-permute-start | bytes 2359304 | tf_op jit(solution)/shard_map/ppermute | solution.py:389
